TPU v7x, 512 devices: a whole 4x8x8 slice. The times are simulated.
512 devices in a mesh: dp: 8 (over z_hi, core), seq: 64 (over z_lo, x, y).
Axes of the slice: x: 4, y: 8, z: 8 (z_hi: 4, z_lo: 2; z = z_hi * 2 + z_lo), core: 2. Of those that a mesh axis runs over, the one named last changes fastest.
Arguments:
- features: bfloat16 [8, 8192, 512], P('dp', 'seq'), may hold values from -40 to 40
- score_cotangent: float32 [8, 8192], P('dp', 'seq'), may hold values from -24 to 24
- projection_weight: bfloat16 [512, 768], replicated, may hold values from -0.25 to 0.25
- squeeze_weight: bfloat16 [64, 768], replicated, may hold values from -0.21875 to 0.21875
- first_weight: bfloat16 [320, 128], replicated, may hold values from -0.3125 to 0.3125
- second_weight: bfloat16 [640, 256], replicated, may hold values from -0.25 to 0.25
- third_weight: bfloat16 [1280, 256], replicated, may hold values from -0.15625 to 0.15625
- final_weight: bfloat16 [768], replicated, may hold values from -0.875 to 0.875
Outputs:
- scores: float32 [8, 8192], P('dp', 'seq')
- feature_grad: float32 [8, 8192, 512], P('dp', 'seq')
- squeeze_grad: float32 [64, 768], P('seq')
- first_grad: float32 [320, 128], P('seq')
- second_grad: float32 [640, 256], P('seq')
- third_grad: float32 [1280, 256], P('seq')
- final_grad: float32 [768], P('seq')
All inputs are finite; a program needn't handle non-finite values.
Results may differ from a plain program's by a relative error of at most 0.025.
Values may be sent and summed in bfloat16 or wider, within the bound.
A program may use at most 64 MiB of HBM per device.

v0:
```python
import math

import jax
import jax.numpy as jnp
from jax import lax
from jax.sharding import PartitionSpec as P

C0 = 64
C1 = 128
C2 = 256
HK = 5
PK = 3


EPSILON = 1e-05
SLOPE = 0.1


def padded(block, sides, width):
    for axis, dim in sides:
        count = lax.axis_size(axis)
        forward = [(i, i + 1) for i in range(count - 1)]
        backward = [(target, source) for source, target in forward]
        low = lax.ppermute(
            lax.slice_in_dim(block, block.shape[dim] - width, None, axis=dim), axis, forward
        )
        high = lax.ppermute(lax.slice_in_dim(block, 0, width, axis=dim), axis, backward)
        block = jnp.concatenate([low, block, high], axis=dim)
    return block


def normalize(values):
    average = jnp.mean(values, axis=-1, keepdims=True)
    centred = values - average
    variance = jnp.mean(centred * centred, axis=-1, keepdims=True)
    inverse = lax.rsqrt(variance + EPSILON)
    return (centred * inverse, inverse)


def normalize_back(upstream, normed, inverse):
    first_mean = jnp.mean(upstream, axis=-1, keepdims=True)
    second_mean = jnp.mean(upstream * normed, axis=-1, keepdims=True)
    return (upstream - first_mean - normed * second_mean) * inverse


def gelu_slope(values):
    cumulative = 0.5 * (1.0 + lax.erf(values * math.sqrt(0.5)))
    density = jnp.exp(-0.5 * values * values) / math.sqrt(2.0 * math.pi)
    return cumulative + values * density


def leaky_unit(values):
    return SLOPE * values + (1.0 - SLOPE) * jax.nn.gelu(values, approximate=False)


def leaky_slope(values):
    return SLOPE + (1.0 - SLOPE) * gelu_slope(values)


def convolve(extended, weights):
    return lax.conv_general_dilated(
        extended,
        weights,
        (1,),
        "VALID",
        dimension_numbers=("NWC", "WIO", "NWC"),
        preferred_element_type=jnp.float32,
    )


def flipped_plain(weights):
    return jnp.swapaxes(weights, 1, 2)[::-1]


def tap_gradients(extended, delta):
    length = delta.shape[1]
    pieces = [
        jnp.einsum(
            "utc,ute->ce",
            extended[:, offset : offset + length],
            delta,
            preferred_element_type=jnp.float32,
        )
        for offset in range(HK)
    ]
    return jnp.concatenate(pieces, axis=0)


def shards(
    features,
    score_cotangent,
    projection_weight,
    squeeze_weight,
    first_weight,
    second_weight,
    third_weight,
    final_weight,
):
    frames = features.shape[1]
    head_pad = (HK - 1) // 2
    final_pad = (PK - 1) // 2
    normed_in, inverse_in = normalize(features.astype(jnp.float32))
    rounded_in = normed_in.astype(jnp.bfloat16)
    projected = jnp.einsum(
        "utf,fd->utd", rounded_in, projection_weight, preferred_element_type=jnp.float32
    ).astype(jnp.bfloat16)
    hidden_normed, hidden_inverse = normalize(projected.astype(jnp.float32))
    hidden = hidden_normed.astype(jnp.bfloat16)
    squeezed = jnp.einsum("utd,cd->utc", hidden, squeeze_weight, preferred_element_type=jnp.float32)
    kernel_one = first_weight.reshape(HK, C0, C1)
    kernel_two = second_weight.reshape(HK, C1, C2)
    kernel_three = third_weight.reshape(HK, C2, C2)
    first_ext = padded(leaky_unit(squeezed).astype(jnp.bfloat16), (("seq", 1),), head_pad)
    first_act = convolve(first_ext, kernel_one)
    second_ext = padded(leaky_unit(first_act).astype(jnp.bfloat16), (("seq", 1),), head_pad)
    second_act = convolve(second_ext, kernel_two)
    third_ext = padded(leaky_unit(second_act).astype(jnp.bfloat16), (("seq", 1),), head_pad)
    third_act = convolve(third_ext, kernel_three)
    final_ext = padded(leaky_unit(third_act).astype(jnp.bfloat16), (("seq", 1),), final_pad)
    scores = convolve(final_ext, final_weight.reshape(PK, C2, 1))[:, :, 0]
    cotangent_ext = padded(score_cotangent, (("seq", 1),), final_pad)
    final_taps = final_weight.astype(jnp.float32).reshape(PK, C2)
    upstream = jnp.zeros(third_act.shape, jnp.float32)
    for offset in range(PK):
        upstream = (
            upstream
            + cotangent_ext[:, offset : offset + frames, None] * final_taps[PK - 1 - offset]
        )
    final_grad = jnp.concatenate(
        [
            jnp.einsum(
                "ut,utc->c",
                score_cotangent,
                final_ext[:, offset : offset + frames].astype(jnp.float32),
                precision=lax.Precision.HIGHEST,
            )
            for offset in range(PK)
        ],
        axis=0,
    )
    delta_three = (upstream * leaky_slope(third_act)).astype(jnp.bfloat16)
    third_grad = tap_gradients(third_ext, delta_three)
    delta_three_ext = padded(delta_three, (("seq", 1),), head_pad)
    upstream = convolve(delta_three_ext, flipped_plain(kernel_three))
    delta_two = (upstream * leaky_slope(second_act)).astype(jnp.bfloat16)
    second_grad = tap_gradients(second_ext, delta_two)
    delta_two_ext = padded(delta_two, (("seq", 1),), head_pad)
    upstream = convolve(delta_two_ext, flipped_plain(kernel_two))
    delta_one = (upstream * leaky_slope(first_act)).astype(jnp.bfloat16)
    first_grad = tap_gradients(first_ext, delta_one)
    delta_one_ext = padded(delta_one, (("seq", 1),), head_pad)
    upstream = convolve(delta_one_ext, flipped_plain(kernel_one))
    delta_squeeze = (upstream * leaky_slope(squeezed)).astype(jnp.bfloat16)
    squeeze_grad = jnp.einsum(
        "utc,utd->cd", delta_squeeze, hidden, preferred_element_type=jnp.float32
    )
    hidden_upstream = jnp.einsum(
        "utc,cd->utd", delta_squeeze, squeeze_weight, preferred_element_type=jnp.float32
    )
    projected_grad = normalize_back(hidden_upstream, hidden_normed, hidden_inverse).astype(
        jnp.bfloat16
    )
    normed_grad = jnp.einsum(
        "utd,fd->utf", projected_grad, projection_weight, preferred_element_type=jnp.float32
    )
    feature_grad = normalize_back(normed_grad, normed_in, inverse_in)
    factor = 1.0 / math.sqrt(lax.axis_size("dp") * lax.axis_size("seq") * frames)
    terms = (
        squeeze_grad * factor,
        first_grad * factor,
        second_grad * factor,
        third_grad * factor,
        final_grad * factor,
    )
    totals = lax.psum((terms[0], terms[1], terms[2], terms[3], terms[4]), ("dp", "seq"))
    position = lax.axis_index("seq")
    width_seq = lax.axis_size("seq")
    shares = tuple(
        (
            lax.dynamic_slice_in_dim(
                summand,
                position * (summand.shape[0] // width_seq),
                summand.shape[0] // width_seq,
                0,
            )
            for summand in totals
        )
    )
    return (scores, feature_grad, shares[0], shares[1], shares[2], shares[3], shares[4])


def solution(mesh):
    placed = (P("dp", "seq", None), P("dp", "seq"), P(), P(), P(), P(), P(), P())
    return jax.shard_map(
        shards,
        mesh=mesh,
        in_specs=placed,
        out_specs=(
            P("dp", "seq"),
            P("dp", "seq", None),
            P("seq", None),
            P("seq", None),
            P("seq", None),
            P("seq", None),
            P("seq"),
        ),
        check_vma=False,
    )
```

profile of v0, /device:TPU:1, one launch (start us, length us, event | category | flops | bytes accessed | tf_op | source)
XLA Modules:
  0.0 505.2 jit_solution(9020769134700706410)
XLA Ops:
  7.2 1.3 fusion.319
  8.6 4.5 collective-permute-start.8
  13.1 1.3 collective-permute-start.9
  15.4 1.1 fusion.14
  16.5 1.3 fusion.320
  18.5 4.0 collective-permute-start
  22.5 1.3 collective-permute-start.1
  23.9 3.1 collective-permute-done.1
  28.3 3.6 collective-permute-start.2
  32.0 1.3 collective-permute-start.3
  33.3 4.2 collective-permute-done.3
  38.2 4.6 collective-permute-start.4
  42.8 1.3 collective-permute-start.5
  44.1 1.3 fusion.256
  45.4 1.7 collective-permute-done.5
  48.3 3.4 collective-permute-start.10
  51.7 1.3 collective-permute-start.11
  53.0 4.0 collective-permute-start.6
  57.0 1.3 collective-permute-start.7
  59.4 1.1 broadcast_multiply_fusion
  62.7 126.0 %psum.39 = f32[768]{0:T(1024)S(1)} all-reduce(f32[768]{0:T(1024)S(1)} %maximum_multiply_fusion), channel_id=1, replica_groups=mesh['dp'=8,'seq'=64] {'dp','seq'}, use_global_device_ids=true, to_apply=%region_12.0 | all-reduce | flops 768 | bytes 6144 | tf_op jit(solution)/shard_map/psum | solution.py:175
  189.9 1.3 collective-permute-start.12
  191.2 1.3 collective-permute-start.13
  194.4 1.1 collective-permute-done.13
  196.0 2.9 collective-permute-start.14
  198.9 1.3 collective-permute-start.15
  201.8 1.4 collective-permute-done.15
  207.2 285.9 %all-reduce.3.cloned.1.call-done = (f32[64,768]{1,0:T(8,128)}, f32[320,128]{1,0:T(8,128)}, f32[640,256]{1,0:T(8,128)}, f32[1280,256]{1,0:T(8,128)}) async-done(((f32[64,768]{1,0:T(8,128)}, f32[320,128]{1,0:T(8,128)}, f32[640,256]{1,0:T(8,128)}, f32[1280,256]{1,0:T(8,128)}), (f32[64,768]{1,0:T(8,128)}, f32[320,128]{1,0:T(8,128)}, f32[640,256]{1,0:T(8,128)}, ...) | async-done | bytes 2326544 | tf_op jit(solution)/shard_map/psum | solution.py:175
  493.0 1.3 constant_dynamic-slice_fusion.3
  494.4 1.3 constant_dynamic-slice_fusion.2
  495.7 1.3 constant_dynamic-slice_fusion.1
  497.0 1.4 constant_dynamic-slice_fusion
  (144 shorter events, 16.9 us)
Async XLA Ops:
  7.2 9.3 %copy-start = (bf16[512,768]{1,0:T(8,128)(2,1)S(1)}, bf16[512,768]{1,0:T(8,128)(2,1)}, u32[]{:S(2)}) copy-start(bf16[512,768]{1,0:T(8,128)(2,1)} %param.10) | copy-start | bytes 2359300
  7.2 11.0 %copy-start.2 = (bf16[64,768]{1,0:T(8,128)(2,1)S(1)}, bf16[64,768]{1,0:T(8,128)(2,1)}, u32[]{:S(2)}) copy-start(bf16[64,768]{1,0:T(8,128)(2,1)} %param.11) | copy-start | bytes 294916
  7.2 485.8 %all-reduce.3.cloned.1.call-start = ((), (), s32[]{:S(2)}) async-start(), calls=%async_computation | async-start | bytes 4653056 | tf_op jit(solution)/shard_map/psum | solution.py:175
  8.6 35.5 %collective-permute-start.8 = (f32[1,1]{1,0:T(1,128)}, f32[1,1]{1,0:T(1,128)}, u32[]{:S(2)}, u32[]{:S(2)}) collective-permute-start(f32[1,1]{1,0:T(1,128)} %get-tuple-element.34), channel_id=1, source_target_pairs={{0,1},{1,2},{2,3},{3,4},{4,5},{5,6},{6,7},{7,8},{8,9},{9,10},{10,1... | collective-permute-start | bytes 20 | tf_op jit(solution)/shard_map/ppermute | solution.py:24
  13.1 31.0 %collective-permute-start.9 = (f32[1,1]{1,0:T(1,128)}, f32[1,1]{1,0:T(1,128)}, u32[]{:S(2)}, u32[]{:S(2)}) collective-permute-start(f32[1,1]{1,0:T(1,128)} %get-tuple-element.35), channel_id=1, source_target_pairs={{1,0},{2,1},{3,2},{4,3},{5,4},{6,5},{7,6},{8,7},{9,8},{10,9},{11,1... | collective-permute-start | bytes 20 | tf_op jit(solution)/shard_map/ppermute | solution.py:27
  17.8 6.0 %copy-start.4 = (bf16[768]{0:T(1024)(128)(2,1)S(1)}, bf16[768]{0:T(1024)(128)(2,1)}, u32[]{:S(2)}) copy-start(bf16[768]{0:T(1024)(128)(2,1)} %param.15) | copy-start | bytes 4612
  17.8 9.5 %copy-start.7 = (bf16[320,128]{1,0:T(8,128)(2,1)S(1)}, bf16[320,128]{1,0:T(8,128)(2,1)}, u32[]{:S(2)}) copy-start(bf16[320,128]{1,0:T(8,128)(2,1)} %param.12) | copy-start | bytes 245764
  17.8 9.5 %copy-start.9 = (pred[8,17]{0,1:T(8,128)(4,1)S(1)}, pred[8,17]{0,1:T(8,128)(4,1)}, u32[]{:S(2)}) copy-start(pred[8,17]{0,1:T(8,128)(4,1)} %constant.44) | copy-start | bytes 412
  18.5 5.3 %collective-permute-start = (bf16[1,2,64]{1,2,0:T(8,128)(2,1)S(1)}, bf16[1,2,64]{1,2,0:T(8,128)(2,1)S(1)}, u32[]{:S(2)}, u32[]{:S(2)}) collective-permute-start(bf16[1,2,64]{1,2,0:T(8,128)(2,1)S(1)} %get-tuple-element.27), channel_id=1, source_target_pairs={{0,1},{1,2},{2,3},{3,4},{4,5},{5,6},{6,7},{7,8},{8,9},{9,10},{10,1... | collective-permute-start | bytes 776 | tf_op jit(solution)/shard_map/ppermute | solution.py:24
  22.5 4.5 collective-permute-start.1
  27.2 10.3 %copy-start.6 = (bf16[640,256]{1,0:T(8,128)(2,1)S(1)}, bf16[640,256]{1,0:T(8,128)(2,1)}, u32[]{:S(2)}) copy-start(bf16[640,256]{1,0:T(8,128)(2,1)} %param.13) | copy-start | bytes 983044
  28.3 4.9 collective-permute-start.2
  32.0 5.5 %collective-permute-start.3 = (bf16[1,2,128]{2,1,0:T(2,128)(2,1)S(1)}, bf16[1,2,128]{2,1,0:T(2,128)(2,1)S(1)}, u32[]{:S(2)}, u32[]{:S(2)}) collective-permute-start(bf16[1,2,128]{2,1,0:T(2,128)(2,1)S(1)} %get-tuple-element.26), channel_id=1, source_target_pairs={{1,0},{2,1},{3,2},{4,3},{5,4},{6,5},{7,6},{8,7},{9,8},{10,9},{11,1... | collective-permute-start | bytes 1544 | tf_op jit(solution)/shard_map/ppermute | solution.py:27
  37.6 6.5 %copy-start.3 = (f32[1,128]{1,0:T(1,128)S(1)}, f32[1,128]{1,0:T(1,128)}, u32[]{:S(2)}) copy-start(f32[1,128]{1,0:T(1,128)} %param.9) | copy-start | bytes 1540
  37.6 9.6 %copy-start.5 = (bf16[1280,256]{1,0:T(8,128)(2,1)S(1)}, bf16[1280,256]{1,0:T(8,128)(2,1)}, u32[]{:S(2)}) copy-start(bf16[1280,256]{1,0:T(8,128)(2,1)} %param.14) | copy-start | bytes 1966084
  38.2 7.2 %collective-permute-start.4 = (bf16[1,2,256]{2,1,0:T(2,128)(2,1)S(1)}, bf16[1,2,256]{2,1,0:T(2,128)(2,1)S(1)}, u32[]{:S(2)}, u32[]{:S(2)}) collective-permute-start(bf16[1,2,256]{2,1,0:T(2,128)(2,1)S(1)} %get-tuple-element.19), channel_id=1, source_target_pairs={{0,1},{1,2},{2,3},{3,4},{4,5},{5,6},{6,7},{7,8},{8,9},{9,10},{10,1... | collective-permute-start | bytes 3080 | tf_op jit(solution)/shard_map/ppermute | solution.py:24
  42.8 4.3 collective-permute-start.5
  48.3 141.0 %collective-permute-start.10 = (bf16[1,2,256]{2,1,0:T(2,128)(2,1)S(1)}, bf16[1,2,256]{2,1,0:T(2,128)(2,1)S(1)}, u32[]{:S(2)}, u32[]{:S(2)}) collective-permute-start(bf16[1,2,256]{2,1,0:T(2,128)(2,1)S(1)} %get-tuple-element.21), channel_id=1, source_target_pairs={{0,1},{1,2},{2,3},{3,4},{4,5},{5,6},{6,7},{7,8},{8,9},{9,10},{10,1... | collective-permute-start | bytes 3080 | tf_op jit(solution)/shard_map/ppermute | solution.py:24
  51.7 137.6 %collective-permute-start.11 = (bf16[1,2,256]{2,1,0:T(2,128)(2,1)S(1)}, bf16[1,2,256]{2,1,0:T(2,128)(2,1)S(1)}, u32[]{:S(2)}, u32[]{:S(2)}) collective-permute-start(bf16[1,2,256]{2,1,0:T(2,128)(2,1)S(1)} %get-tuple-element.22), channel_id=1, source_target_pairs={{1,0},{2,1},{3,2},{4,3},{5,4},{6,5},{7,6},{8,7},{9,8},{10,9},{11,1... | collective-permute-start | bytes 3080 | tf_op jit(solution)/shard_map/ppermute | solution.py:27
  53.0 7.5 %collective-permute-start.6 = (bf16[1,1,256]{2,1,0:T(2,128)(2,1)S(1)}, bf16[1,1,256]{2,1,0:T(2,128)(2,1)S(1)}, u32[]{:S(2)}, u32[]{:S(2)}) collective-permute-start(bf16[1,1,256]{2,1,0:T(2,128)(2,1)S(1)} %get-tuple-element.17), channel_id=1, source_target_pairs={{0,1},{1,2},{2,3},{3,4},{4,5},{5,6},{6,7},{7,8},{8,9},{9,10},{10,1... | collective-permute-start | bytes 1544 | tf_op jit(solution)/shard_map/ppermute | solution.py:24
  57.0 4.3 collective-permute-start.7
  59.4 2.0 copy-start.8
  189.9 4.5 collective-permute-start.12
  191.2 4.3 collective-permute-start.13
  192.9 2.7 copy-start.10
  196.0 5.8 %collective-permute-start.14 = (bf16[1,2,128]{2,1,0:T(2,128)(2,1)S(1)}, bf16[1,2,128]{2,1,0:T(2,128)(2,1)S(1)}, u32[]{:S(2)}, u32[]{:S(2)}) collective-permute-start(bf16[1,2,128]{2,1,0:T(2,128)(2,1)S(1)} %get-tuple-element.23), channel_id=1, source_target_pairs={{0,1},{1,2},{2,3},{3,4},{4,5},{5,6},{6,7},{7,8},{8,9},{9,10},{10,1... | collective-permute-start | bytes 1544 | tf_op jit(solution)/shard_map/ppermute | solution.py:24
  198.9 4.3 collective-permute-start.15
  204.8 0.9 copy-start.1
Sparse Core Ops, SparseCore 0:
  205.0 288.0 all-reduce.2
where the time goes:
time: 506 us; the launch traced here: 505 us
  waiting for transfers between devices  298 us (59%)
  blocking collectives  126 us (25%)
  starting transfers between devices  38.6 us (8%)
  between operations  14.9 us (3%)
  local copies, waits for them, and re-layouts  9.99 us (2%)
  matrix products  9.75 us (2%)
  other arithmetic  7.74 us (2%)
    psum x1, waiting for transfers between devices, shards(): lax.psum((terms[0], terms[1], terms[2], terms[3], terms[4]), ('dp', 'seq'))  286 us
    psum x1, blocking collectives, shards(): lax.psum((terms[0], terms[1], terms[2], terms[3], terms[4]), ('dp', 'seq'))  126 us
    ppermute x8, starting transfers between devices, padded(): lax.ppermute(lax.slice_in_dim(block, block.shape[dim] - width, None, axis...  28.2 us
    ppermute x8, waiting for transfers between devices, padded(): lax.ppermute(lax.slice_in_dim(block, 0, width, axis=dim), axis, backward)  12.3 us
    ppermute x8, starting transfers between devices, padded(): lax.ppermute(lax.slice_in_dim(block, 0, width, axis=dim), axis, backward)  10.3 us
  transfers between devices with their start and end apart: 17, of which 7 were waited for; matrix products, arithmetic and copies ran while one was open for 3% of the time, Pallas kernels for 0%

commit v1 on v0

v1 whole, which is shorter than its diff:
```python
import math

import jax
import jax.numpy as jnp
from jax import lax
from jax.experimental import pallas as pl
from jax.experimental.pallas import tpu as pltpu
from jax.sharding import PartitionSpec as P

MESH = pl.DeviceIdType.MESH
F32 = jnp.float32
BF16 = jnp.bfloat16

C0, C1, C2 = 64, 128, 256
HK, PK = 5, 3
EPSILON = 1e-05
SLOPE = 0.1
FRAMES = 128
HALO = 16
ROWS = FRAMES + 2 * HALO
OWN = slice(HALO, HALO + FRAMES)

ZH, CORES, ZL, NX, NY = 4, 2, 2, 4, 8
NZ = ZH * ZL
SHARES = ZL * NX * NY
TROWS, RROWS = 24, 16


def dot(a, b, ca=1, cb=0):
    return lax.dot_general(a, b, (((ca,), (cb,)), ((), ())), preferred_element_type=F32)


def normalize(values):
    average = jnp.mean(values, axis=-1, keepdims=True)
    centred = values - average
    variance = jnp.mean(centred * centred, axis=-1, keepdims=True)
    inverse = lax.rsqrt(variance + EPSILON)
    return centred * inverse, inverse


def normalize_back(upstream, normed, inverse):
    first_mean = jnp.mean(upstream, axis=-1, keepdims=True)
    second_mean = jnp.mean(upstream * normed, axis=-1, keepdims=True)
    return (upstream - first_mean - normed * second_mean) * inverse


def activation(v):
    cumulative = 0.5 * (1.0 + lax.erf(v * math.sqrt(0.5)))
    density = jnp.exp(-0.5 * v * v) * (1.0 / math.sqrt(2.0 * math.pi))
    value = SLOPE * v + (1.0 - SLOPE) * (v * cumulative)
    slope = SLOPE + (1.0 - SLOPE) * (cumulative + v * density)
    return value, slope


def shifted(v, shift):
    return pltpu.roll(v, (-shift) % v.shape[0], 0) if shift else v


def split3(v):
    hi = v.astype(BF16).astype(F32)
    mid = (v - hi).astype(BF16).astype(F32)
    return hi, mid, (v - hi - mid).astype(BF16).astype(F32)


def kernel(
    feat, cot, wp, ws, w1, w2, w3, wf,
    scores, fgrad, sq_out, g1_out, g2_out, g3_out, gf_out,
    hfeat, hcot, xr, x2, x3, cots, wfs, g3s, g2s, g1s, tst, rst,
    tb, rb, t0, r0, t1, r1, tx, ry, t2, r2, ty, rx, zs, zr, fin,
    hs, hr, s0, q0, sx, qx, sy, qy, sy2, qy2, sx2, qx2, sz, qz, s4, q4,
):
    dp, sq = lax.axis_index("dp"), lax.axis_index("seq")
    zh, core = dp // CORES, dp % CORES
    zl, px, py = sq // (NX * NY), (sq // NY) % NX, sq % NY
    pz = zh * ZL + zl
    count = SHARES

    def at(z=None, x=None, y=None, c=None):
        z = pz if z is None else z
        x = px if x is None else x
        y = py if y is None else y
        c = core if c is None else c
        return ((z // ZL) * CORES + c, (z % ZL) * NX * NY + x * NY + y)

    before = (dp, (sq + count - 1) % count)
    after = (dp, (sq + 1) % count)
    partner = at(c=1 - core)
    peers = [before, after, partner]
    peers += [at(x=(px + d) % NX) for d in range(1, NX)]
    peers += [at(y=(py + d) % NY) for d in range(1, NY)]
    peers += [at(z=(pz + d) % NZ) for d in range(1, NZ)]

    barrier = pltpu.get_barrier_semaphore()
    for peer in peers:
        pl.semaphore_signal(barrier, inc=1, device_id=peer, device_id_type=MESH)
    pl.semaphore_wait(barrier, len(peers))

    def send(src, dst, ss, rs, peer):
        copy = pltpu.make_async_remote_copy(
            src_ref=src, dst_ref=dst, send_sem=ss, recv_sem=rs, device_id=peer, device_id_type=MESH
        )
        copy.start()
        return copy

    halo = [
        send(feat.at[0, pl.ds(FRAMES - HALO, HALO)], hfeat.at[0], hs.at[0], hr.at[0], after),
        send(feat.at[0, pl.ds(0, HALO)], hfeat.at[1], hs.at[1], hr.at[1], before),
        send(cot, hcot.at[0], hs.at[2], hr.at[2], after),
        send(cot, hcot.at[1], hs.at[3], hr.at[3], before),
    ]

    has_low, has_high = sq > 0, sq < count - 1
    row = lax.broadcasted_iota(jnp.int32, (ROWS, 1), 0)
    first_row = jnp.where(has_low, 0, HALO)
    last_row = jnp.where(has_high, ROWS, HALO + FRAMES)
    inside = jnp.logical_and(row >= first_row, row < last_row)

    def masked(v):
        return jnp.where(inside, v, 0.0)

    normed_in, inverse_in = normalize(feat[0].astype(F32))
    xr[OWN] = normed_in.astype(BF16)
    for copy in halo:
        copy.wait()
    edge = jnp.concatenate(
        [
            jnp.where(has_low, hfeat[0].astype(F32), 0.0),
            jnp.where(has_high, hfeat[1].astype(F32), 0.0),
        ],
        axis=0,
    )
    edge = normalize(edge)[0].astype(BF16)
    xr[0:HALO] = edge[0:HALO]
    xr[HALO + FRAMES : ROWS] = edge[HALO:]

    projected = dot(xr[...], wp[...]).astype(BF16)
    hidden_all, hidden_inverse = normalize(projected.astype(F32))
    hidden = hidden_all.astype(BF16)
    hidden_normed, hidden_inverse = hidden_all[OWN], hidden_inverse[OWN]
    squeezed = dot(hidden, ws[...], 1, 1)
    hidden = hidden[OWN]

    v1, squeezed_slope = activation(squeezed)
    v1 = v1.astype(BF16).astype(F32)
    taps1 = [shifted(v1, k - 2).astype(BF16) for k in range(HK)]
    first_act = sum(dot(taps1[k], w1[k * C0 : (k + 1) * C0]) for k in range(HK))

    v2, slope1 = activation(first_act)
    v2 = masked(v2)
    for k in range(HK):
        x2[:, k * C1 : (k + 1) * C1] = shifted(v2, k - 2).astype(BF16)
    second_act = dot(x2[...], w2[...])

    v3, slope2 = activation(second_act)
    v3 = masked(v3)
    for k in range(HK):
        x3[:, k * C2 : (k + 1) * C2] = shifted(v3, k - 2).astype(BF16)
    third_act = dot(x3[...], w3[...])

    v4, slope3 = activation(third_act)
    v4 = masked(v4)
    final_taps = [shifted(v4, k - 1)[OWN].astype(BF16) for k in range(PK)]
    wrow = [wf[k : k + 1, :] for k in range(PK)]
    total = sum(dot(jnp.broadcast_to(wrow[k], (8, C2)), final_taps[k], 1, 1) for k in range(PK))
    scores[...] = total[0:1]

    low = jnp.where(has_low, hcot[0], 0.0)
    high = jnp.where(has_high, hcot[1], 0.0)
    line = jnp.concatenate([low, cot[...], high], axis=1)
    cots[...] = jnp.zeros_like(cots)
    wfs[...] = jnp.zeros_like(wfs)
    pieces = split3(line)
    for p in range(3):
        for k in range(PK):
            start = FRAMES - HALO - k + 1
            cots[3 * k + p : 3 * k + p + 1, :] = pltpu.roll(pieces[p], 3 * FRAMES - start, 1)[:, : 2 * FRAMES]
            wfs[3 * k + p : 3 * k + p + 1, :] = wrow[k].astype(F32)
        cots[16 + p : 17 + p, 0:FRAMES] = pieces[p][:, FRAMES : 2 * FRAMES]
    upstream = dot(cots[0:16].astype(BF16), wfs[...].astype(BF16), 0, 0)[:ROWS]
    own_cot = cots[16:24, 0:FRAMES].astype(BF16)
    final_grad = [
        jnp.sum(dot(own_cot, final_taps[k]), axis=0, keepdims=True) for k in range(PK)
    ]

    delta = masked(upstream * slope3).astype(BF16)
    grad = dot(x3[OWN], delta[OWN], 0, 0)
    g3s[0], g3s[1] = grad[:, :128], grad[:, 128:]
    for h in range(CORES):
        for r in range(20):
            tst.at[h][pl.ds(r, SHARES, stride=TROWS), :] = g3s.at[h][pl.ds(r, SHARES, stride=20), :]
        for r in range(20, TROWS):
            tst.at[h][pl.ds(r, SHARES, stride=TROWS), :] = jnp.zeros((SHARES, 128), F32)
        for s in range(SHARES):
            a, b, c = s // (NX * NY), (s // NY) % NX, s % NY
            tb[h, b, c, a] = tst[h, s * TROWS : (s + 1) * TROWS].astype(BF16)
    core_t = send(tb.at[1 - core], t0, s0.at[0], q0.at[0], partner)

    def back(delta, weight, width):
        d = delta.astype(F32)
        return sum(
            dot(shifted(d, 2 - k).astype(BF16), weight[k * width : (k + 1) * width], 1, 1)
            for k in range(HK)
        )

    upstream = back(delta, w3, C2)
    delta = masked(upstream * slope2).astype(BF16)
    grad = dot(x2[OWN], delta[OWN], 0, 0)
    g2s[0], g2s[1] = grad[:, :128], grad[:, 128:]
    for h in range(CORES):
        for r in range(10):
            rst.at[h][pl.ds(r, SHARES, stride=RROWS), :] = g2s.at[h][pl.ds(r, SHARES, stride=10), :]

    upstream = back(delta, w2, C1)
    delta = masked(upstream * slope1).astype(BF16)
    for k in range(HK):
        g1s[k * C0 : (k + 1) * C0] = dot(taps1[k][OWN], delta[OWN], 0, 0)
    for r in range(5):
        rst.at[1][pl.ds(10 + r, SHARES, stride=RROWS), :] = g1s[pl.ds(r, SHARES, stride=5), :]

    flat = jnp.concatenate(final_grad, axis=1)
    width = (PK * C2) // SHARES
    offset = lax.broadcasted_iota(jnp.int32, (SHARES, PK * C2), 1) - width * lax.broadcasted_iota(
        jnp.int32, (SHARES, PK * C2), 0
    )
    picked = jnp.where(jnp.logical_and(offset >= 0, offset < width), flat, 0.0).astype(BF16)
    place = lax.broadcasted_iota(jnp.int32, (PK * C2, 128), 0)
    place = place - width * ((place * 5462) >> 16) - lax.broadcasted_iota(jnp.int32, (PK * C2, 128), 1)
    spread = jnp.where(place == 0, 1.0, 0.0).astype(BF16)
    rst.at[1][pl.ds(15, SHARES, stride=RROWS), :] = dot(picked, spread)

    upstream = back(delta, w1, C0)
    delta_squeeze = (upstream[OWN] * squeezed_slope[OWN]).astype(BF16)
    grad = dot(delta_squeeze, hidden, 0, 0)
    for j in range(6):
        rst.at[0][pl.ds(10 + j, SHARES, stride=RROWS), :] = grad[:, j * 128 : (j + 1) * 128]
    for h in range(CORES):
        for s in range(SHARES):
            a, b, c = s // (NX * NY), (s // NY) % NX, s % NY
            rb[h, c, b, a] = rst[h, s * RROWS : (s + 1) * RROWS].astype(BF16)
    core_r = send(rb.at[1 - core], r0, s0.at[1], q0.at[1], partner)

    core_t.wait()
    t1[...] = (tb[core].astype(F32) + t0[...].astype(F32)).astype(BF16)
    along_x = [
        send(t1.at[(px + d) % NX], tx.at[d - 1], sx.at[d - 1], qx.at[d - 1], at(x=(px + d) % NX))
        for d in range(1, NX)
    ]
    core_r.wait()
    r1[...] = (rb[core].astype(F32) + r0[...].astype(F32)).astype(BF16)
    along_y = [
        send(r1.at[(py + d) % NY], ry.at[d - 1], sy.at[d - 1], qy.at[d - 1], at(y=(py + d) % NY))
        for d in range(1, NY)
    ]

    hidden_upstream = dot(delta_squeeze, ws[...])
    projected_grad = normalize_back(hidden_upstream, hidden_normed, hidden_inverse).astype(BF16)
    normed_grad = dot(projected_grad, wp[...], 1, 1)
    fgrad[0] = normalize_back(normed_grad, normed_in, inverse_in)

    for copy in along_x:
        copy.wait()
    acc = t1[px].astype(F32)
    for d in range(NX - 1):
        acc = acc + tx[d].astype(F32)
    t2[...] = acc.astype(BF16)
    along_y2 = [
        send(t2.at[(py + d) % NY], ty.at[d - 1], sy2.at[d - 1], qy2.at[d - 1], at(y=(py + d) % NY))
        for d in range(1, NY)
    ]
    for copy in along_y:
        copy.wait()
    acc = r1[py].astype(F32)
    for d in range(NY - 1):
        acc = acc + ry[d].astype(F32)
    r2[...] = acc.astype(BF16)
    along_x2 = [
        send(r2.at[(px + d) % NX], rx.at[d - 1], sx2.at[d - 1], qx2.at[d - 1], at(x=(px + d) % NX))
        for d in range(1, NX)
    ]
    for copy in along_x2:
        copy.wait()
    acc = r2[px].astype(F32)
    for d in range(NX - 1):
        acc = acc + rx[d].astype(F32)
    zs[:, TROWS:] = acc.astype(BF16)
    for copy in along_y2:
        copy.wait()
    acc = t2[py].astype(F32)
    for d in range(NY - 1):
        acc = acc + ty[d].astype(F32)
    zs[:, :TROWS] = acc.astype(BF16)

    along_z = []
    for d in range(1, NZ):
        target = (pz + d) % NZ
        along_z.append(send(zs.at[target % ZL], zr.at[d], sz.at[d - 1], qz.at[d - 1], at(z=target)))
    for copy in along_z:
        copy.wait()
    zr[0] = zs[zl]
    acc = jnp.zeros((TROWS + RROWS, 128), F32)
    for z in range(NZ):
        acc = acc + zr[(pz + NZ - z) % NZ].astype(F32)
    fin[core] = acc * (1.0 / math.sqrt(FRAMES * SHARES * ZH * CORES))
    send(fin.at[core], fin.at[core], s4, q4, partner).wait()

    g3_out[...] = jnp.concatenate([fin[0, 0:20], fin[1, 0:20]], axis=1)
    g2_out[...] = jnp.concatenate([fin[0, 24:34], fin[1, 24:34]], axis=1)
    g1_out[...] = fin[1, 34:39]
    gf_out[...] = fin[1, 39:40]
    for j in range(6):
        sq_out[:, j * 128 : (j + 1) * 128] = fin[0, 34 + j : 35 + j]


def shards(features, cotangent, wp, ws, w1, w2, w3, wf):
    vmem = pl.BlockSpec(memory_space=pltpu.VMEM)
    dma = pltpu.SemaphoreType.DMA
    outs = pl.pallas_call(
        kernel,
        out_shape=(
            jax.ShapeDtypeStruct((1, FRAMES), F32),
            jax.ShapeDtypeStruct((1, FRAMES, 512), F32),
            jax.ShapeDtypeStruct((1, 768), F32),
            jax.ShapeDtypeStruct((5, 128), F32),
            jax.ShapeDtypeStruct((10, 256), F32),
            jax.ShapeDtypeStruct((20, 256), F32),
            jax.ShapeDtypeStruct((1, 128), F32),
        ),
        in_specs=[vmem] * 8,
        out_specs=(vmem,) * 7,
        scratch_shapes=[
            pltpu.VMEM((2, HALO, 512), BF16),
            pltpu.VMEM((2, 1, FRAMES), F32),
            pltpu.VMEM((ROWS, 512), BF16),
            pltpu.VMEM((ROWS, HK * C1), BF16),
            pltpu.VMEM((ROWS, HK * C2), BF16),
            pltpu.VMEM((24, 2 * FRAMES), F32),
            pltpu.VMEM((16, C2), F32),
            pltpu.VMEM((2, HK * C2, 128), F32),
            pltpu.VMEM((2, HK * C1, 128), F32),
            pltpu.VMEM((HK * C0, 128), F32),
            pltpu.VMEM((2, SHARES * TROWS, 128), F32),
            pltpu.VMEM((2, SHARES * RROWS, 128), F32),
            pltpu.VMEM((2, NX, NY, ZL, TROWS, 128), BF16),
            pltpu.VMEM((2, NY, NX, ZL, RROWS, 128), BF16),
            pltpu.VMEM((NX, NY, ZL, TROWS, 128), BF16),
            pltpu.VMEM((NY, NX, ZL, RROWS, 128), BF16),
            pltpu.VMEM((NX, NY, ZL, TROWS, 128), BF16),
            pltpu.VMEM((NY, NX, ZL, RROWS, 128), BF16),
            pltpu.VMEM((NX - 1, NY, ZL, TROWS, 128), BF16),
            pltpu.VMEM((NY - 1, NX, ZL, RROWS, 128), BF16),
            pltpu.VMEM((NY, ZL, TROWS, 128), BF16),
            pltpu.VMEM((NX, ZL, RROWS, 128), BF16),
            pltpu.VMEM((NY - 1, ZL, TROWS, 128), BF16),
            pltpu.VMEM((NX - 1, ZL, RROWS, 128), BF16),
            pltpu.VMEM((ZL, TROWS + RROWS, 128), BF16),
            pltpu.VMEM((NZ, TROWS + RROWS, 128), BF16),
            pltpu.VMEM((2, TROWS + RROWS, 128), F32),
            dma((4,)), dma((4,)),
            dma((2,)), dma((2,)),
            dma((NX - 1,)), dma((NX - 1,)),
            dma((NY - 1,)), dma((NY - 1,)),
            dma((NY - 1,)), dma((NY - 1,)),
            dma((NX - 1,)), dma((NX - 1,)),
            dma((NZ - 1,)), dma((NZ - 1,)),
            dma, dma,
        ],
        compiler_params=pltpu.CompilerParams(collective_id=0, has_side_effects=True),
    )(features, cotangent, wp, ws, w1, w2, w3, wf.reshape(PK, C2))
    scores, fgrad, sq, g1, g2, g3, gf = outs
    return scores, fgrad, sq, g1, g2, g3, gf[0, : (PK * C2) // SHARES]


def solution(mesh):
    placed = (P("dp", "seq", None), P("dp", "seq"), P(), P(), P(), P(), P(), P())
    return jax.shard_map(
        shards,
        mesh=mesh,
        in_specs=placed,
        out_specs=(
            P("dp", "seq"),
            P("dp", "seq", None),
            P("seq", None),
            P("seq", None),
            P("seq", None),
            P("seq", None),
            P("seq"),
        ),
        check_vma=False,
    )
```

time: 506 us -> 53.7 us (0.11)
  waiting for transfers between devices: 298 us -> 0 us
  blocking collectives: 126 us -> 0 us
  Pallas kernels: 0 us -> 45.1 us
  starting transfers between devices: 38.6 us -> 0 us
  between operations: 14.9 us -> 0.66 us
  matrix products: 9.75 us -> 0 us
  other arithmetic: 7.74 us -> 0 us
    psum x1 -> x0, waiting for transfers between devices: 286 us -> none  [shards(): lax.psum((terms[0], terms[1], terms[2], terms[3], terms[4]), ('dp', 'seq'))]
    psum x1 -> x0, blocking collectives: 126 us -> none  [shards(): lax.psum((terms[0], terms[1], terms[2], terms[3], terms[4]), ('dp', 'seq'))]
    pallas_call x0 -> x1, Pallas kernels: none -> 45.1 us  [shards(): pl.pallas_call(kernel, out_shape=(jax.ShapeDtypeStruct((1, FRAMES), F32),...]
    ppermute x16 -> x0, starting transfers between devices: 38.5 us -> none  [the longest x8 28.2 us: padded(): lax.ppermute(lax.slice_in_dim(block, block.shape[dim] - width, None, axis...]
    ppermute x16 -> x0, waiting for transfers between devices: 12.4 us -> none  [the longest x8 12.3 us: padded(): lax.ppermute(lax.slice_in_dim(block, 0, width, axis=dim), axis, backward)]
    dot_general x23 -> x0, matrix products: 6.62 us -> none  [the longest x15 2.96 us: tap_gradients(): jnp.einsum('utc,ute->ce', extended[:, offset:offset + length], delta, pre...]
    dynamic_slice x5 -> x0, local copies, waits for them, and re-layouts: 5.91 us -> none  [shards(): lax.dynamic_slice_in_dim(summand, position * (summand.shape[0] // width_s...]
  transfers between devices with their start and end apart: 17 -> 0, of which waited for: 7 -> 0; matrix products, arithmetic and copies ran while one was open for 3% -> 0% of each run, Pallas kernels for 0% -> 0%
where the time goes in v1:
time: 53.7 us; the launch traced here: 52.9 us
  Pallas kernels  45.1 us (84%)
  local copies, waits for them, and re-layouts  7.2 us (13%)
  between operations  0.66 us (1%)
    pallas_call x1, Pallas kernels, shards(): pl.pallas_call(kernel, out_shape=(jax.ShapeDtypeStruct((1, FRAMES), F32),...  45.1 us
    unnamed x18, local copies, waits for them, and re-layouts  5.42 us
    reshape x1, local copies, waits for them, and re-layouts, shards(): wf.reshape(PK, C2)  1.27 us

profile of v1, /device:TPU:1, one launch (start us, length us, event | category | flops | bytes accessed | tf_op | source)
XLA Modules:
  0.0 52.9 jit_solution(11388605948223179716)
XLA Ops:
  0.6 1.3 %reshape.17.wf = bf16[3,256]{1,0:T(4,128)(2,1)} reshape(bf16[768]{0:T(1024)(128)(2,1)} %param.15) | data formatting | bytes 3072 | tf_op jit(solution)/shard_map/reshape | solution.py:368
  1.9 45.1 %shard_map.135 = (f32[1,128]{1,0:T(1,128)}, f32[1,128,512]{2,1,0:T(8,128)}, f32[1,768]{1,0:T(1,128)}, f32[5,128]{1,0:T(8,128)}, f32[10,256]{1,0:T(8,128)}, /*index=5*/f32[20,256]{1,0:T(8,128)}, f32[1,128]{1,0:T(1,128)}) custom-call(bf16[1,128,512]{2,1,0:T(8,128)(2,1)} %feat.1, f32[1,128]{1,0:T(1,128)} %cot.1, bf16[512,768]{1,0:T(8,128)(2,1)} %wp.1, ...), custom_call_target="tpu_custom_call" | custom-call | tf_op jit(solution)/shard_map/pallas_call | solution.py:317
  47.0 0.0 copy-start.5
  47.0 0.7 %copy-done.5 = f32[1,128]{1,0:T(1,128)S(1)} copy-done((f32[1,128]{1,0:T(1,128)S(1)}, f32[1,128]{1,0:T(1,128)}, u32[]{:S(2)}) %copy-start.5) | copy-done | bytes 536
  47.7 0.0 copy-start.4
  47.7 0.5 slice_bitcast_fusion
  48.2 0.1 copy-done.4
  48.3 0.5 copy.21
  48.8 0.0 copy-start.3
  48.8 0.0 copy-start.2
  48.8 0.0 copy-start.1
  48.8 1.7 %copy.22 = f32[1,128,512]{2,1,0:T(8,128)} copy(f32[1,128,512]{2,1,0:T(8,128)} %get-tuple-element.29) | data formatting | bytes 524288
  50.5 0.0 copy-done.3
  50.5 0.0 copy-start
  50.5 0.6 %copy.23 = f32[1,768]{1,0:T(1,128)} copy(f32[1,768]{1,0:T(1,128)S(1)} %copy-done.3) | data formatting | bytes 6144
  51.1 0.0 copy-done.2
  51.1 0.6 %copy.24 = f32[5,128]{1,0:T(8,128)} copy(f32[5,128]{1,0:T(8,128)S(1)} %copy-done.2) | data formatting | bytes 5120
  51.7 0.0 copy-done.1
  51.7 0.6 %copy.25 = f32[10,256]{1,0:T(8,128)} copy(f32[10,256]{1,0:T(8,128)S(1)} %copy-done.1) | data formatting | bytes 20480
  52.3 0.0 copy-done
  52.3 0.6 %copy.26 = f32[20,256]{1,0:T(8,128)} copy(f32[20,256]{1,0:T(8,128)S(1)} %copy-done) | data formatting | bytes 40960
Async XLA Ops:
  47.0 0.7 %copy-start.5 = (f32[1,128]{1,0:T(1,128)S(1)}, f32[1,128]{1,0:T(1,128)}, u32[]{:S(2)}) copy-start(f32[1,128]{1,0:T(1,128)} %get-tuple-element.20) | copy-start | bytes 1540
  47.7 0.7 %copy-start.4 = (f32[1,128]{1,0:T(1,128)S(1)}, f32[1,128]{1,0:T(1,128)}, u32[]{:S(2)}) copy-start(f32[1,128]{1,0:T(1,128)} %get-tuple-element.28) | copy-start | bytes 1540
  48.8 1.7 %copy-start.3 = (f32[1,768]{1,0:T(1,128)S(1)}, f32[1,768]{1,0:T(1,128)}, u32[]{:S(2)}) copy-start(f32[1,768]{1,0:T(1,128)} %get-tuple-element.30) | copy-start | bytes 9220
  48.8 2.3 %copy-start.2 = (f32[5,128]{1,0:T(8,128)S(1)}, f32[5,128]{1,0:T(8,128)}, u32[]{:S(2)}) copy-start(f32[5,128]{1,0:T(8,128)} %get-tuple-element.31) | copy-start | bytes 7684
  48.8 2.9 %copy-start.1 = (f32[10,256]{1,0:T(8,128)S(1)}, f32[10,256]{1,0:T(8,128)}, u32[]{:S(2)}) copy-start(f32[10,256]{1,0:T(8,128)} %get-tuple-element.32) | copy-start | bytes 30724
  50.5 1.8 %copy-start = (f32[20,256]{1,0:T(8,128)S(1)}, f32[20,256]{1,0:T(8,128)}, u32[]{:S(2)}) copy-start(f32[20,256]{1,0:T(8,128)} %get-tuple-element.33) | copy-start | bytes 61444

commit v2 on v1

--- a/solution.py
+++ b/solution.py
@@ -63,9 +63,10 @@
 
 
 def kernel(
-    feat, cot, wp, ws, w1, w2, w3, wf,
-    scores, fgrad, sq_out, g1_out, g2_out, g3_out, gf_out,
-    hfeat, hcot, xr, x2, x3, cots, wfs, g3s, g2s, g1s, tst, rst,
+    feat_in, cot_in, wp_in, ws_in, w1_in, w2_in, w3_in, wf_in,
+    scores, fgrad, fin_out,
+    feat, cot, wp, ws, w1, w2, w3, wf, in_sem,
+    hfeat, hcot, x2, x3, cots, wfs, g3s, g2s, g1s, tst, rst,
     tb, rb, t0, r0, t1, r1, tx, ry, t2, r2, ty, rx, zs, zr, fin,
     hs, hr, s0, q0, sx, qx, sy, qy, sy2, qy2, sx2, qx2, sz, qz, s4, q4,
 ):
@@ -93,6 +94,13 @@
     barrier = pltpu.get_barrier_semaphore()
     for peer in peers:
         pl.semaphore_signal(barrier, inc=1, device_id=peer, device_id_type=MESH)
+    sources = (feat_in.at[0], cot_in, wp_in, ws_in, w1_in, w2_in, w3_in, wf_in)
+    loads = [
+        pltpu.make_async_copy(source, target, in_sem.at[i])
+        for i, (source, target) in enumerate(zip(sources, (feat, cot, wp, ws, w1, w2, w3, wf)))
+    ]
+    for load in loads:
+        load.start()
     pl.semaphore_wait(barrier, len(peers))
 
     def send(src, dst, ss, rs, peer):
@@ -103,10 +111,10 @@
         return copy
 
     halo = [
-        send(feat.at[0, pl.ds(FRAMES - HALO, HALO)], hfeat.at[0], hs.at[0], hr.at[0], after),
-        send(feat.at[0, pl.ds(0, HALO)], hfeat.at[1], hs.at[1], hr.at[1], before),
-        send(cot, hcot.at[0], hs.at[2], hr.at[2], after),
-        send(cot, hcot.at[1], hs.at[3], hr.at[3], before),
+        send(feat_in.at[0, pl.ds(FRAMES - HALO, HALO)], hfeat.at[0], hs.at[0], hr.at[0], after),
+        send(feat_in.at[0, pl.ds(0, HALO)], hfeat.at[1], hs.at[1], hr.at[1], before),
+        send(cot_in, hcot.at[0], hs.at[2], hr.at[2], after),
+        send(cot_in, hcot.at[1], hs.at[3], hr.at[3], before),
     ]
 
     has_low, has_high = sq > 0, sq < count - 1
@@ -118,8 +126,19 @@
     def masked(v):
         return jnp.where(inside, v, 0.0)
 
-    normed_in, inverse_in = normalize(feat[0].astype(F32))
-    xr[OWN] = normed_in.astype(BF16)
+    def front(rounded):
+        projected = dot(rounded, wp[...]).astype(BF16)
+        normed, inverse = normalize(projected.astype(F32))
+        rounded = normed.astype(BF16)
+        return normed, inverse, rounded, dot(rounded, ws[...], 1, 1)
+
+    loads[0].wait()
+    normed_in, inverse_in = normalize(feat[...].astype(F32))
+    loads[2].wait()
+    loads[3].wait()
+    hidden_normed, hidden_inverse, hidden, squeezed = front(normed_in.astype(BF16))
+    for i in (1, 4, 5, 6, 7):
+        loads[i].wait()
     for copy in halo:
         copy.wait()
     edge = jnp.concatenate(
@@ -129,16 +148,8 @@
         ],
         axis=0,
     )
-    edge = normalize(edge)[0].astype(BF16)
-    xr[0:HALO] = edge[0:HALO]
-    xr[HALO + FRAMES : ROWS] = edge[HALO:]
-
-    projected = dot(xr[...], wp[...]).astype(BF16)
-    hidden_all, hidden_inverse = normalize(projected.astype(F32))
-    hidden = hidden_all.astype(BF16)
-    hidden_normed, hidden_inverse = hidden_all[OWN], hidden_inverse[OWN]
-    squeezed = dot(hidden, ws[...], 1, 1)
-    hidden = hidden[OWN]
+    edge = front(normalize(edge)[0].astype(BF16))[3]
+    squeezed = jnp.concatenate([edge[:HALO], squeezed, edge[HALO:]], axis=0)
 
     v1, squeezed_slope = activation(squeezed)
     v1 = v1.astype(BF16).astype(F32)
@@ -160,7 +171,9 @@
     v4, slope3 = activation(third_act)
     v4 = masked(v4)
     final_taps = [shifted(v4, k - 1)[OWN].astype(BF16) for k in range(PK)]
-    wrow = [wf[k : k + 1, :] for k in range(PK)]
+    wrow = [
+        jnp.concatenate([wf[2 * k : 2 * k + 1, :], wf[2 * k + 1 : 2 * k + 2, :]], axis=1) for k in range(PK)
+    ]
     total = sum(dot(jnp.broadcast_to(wrow[k], (8, C2)), final_taps[k], 1, 1) for k in range(PK))
     scores[...] = total[0:1]
 
@@ -303,34 +316,45 @@
     fin[core] = acc * (1.0 / math.sqrt(FRAMES * SHARES * ZH * CORES))
     send(fin.at[core], fin.at[core], s4, q4, partner).wait()
 
+    fin_out[...] = fin[...]
+
+
+def finish(scores_in, fgrad_in, fin, scores, fgrad, sq_out, g1_out, g2_out, g3_out, gf_out):
+    scores[...] = scores_in[...]
+    fgrad[...] = fgrad_in[...]
     g3_out[...] = jnp.concatenate([fin[0, 0:20], fin[1, 0:20]], axis=1)
     g2_out[...] = jnp.concatenate([fin[0, 24:34], fin[1, 24:34]], axis=1)
     g1_out[...] = fin[1, 34:39]
-    gf_out[...] = fin[1, 39:40]
+    gf_out[...] = fin[1, 39:40].reshape(128)[: (PK * C2) // SHARES]
     for j in range(6):
         sq_out[:, j * 128 : (j + 1) * 128] = fin[0, 34 + j : 35 + j]
 
 
 def shards(features, cotangent, wp, ws, w1, w2, w3, wf):
     vmem = pl.BlockSpec(memory_space=pltpu.VMEM)
+    operands = (features, cotangent, wp, ws, w1, w2, w3, wf.reshape(6, 128))
     dma = pltpu.SemaphoreType.DMA
     outs = pl.pallas_call(
         kernel,
         out_shape=(
             jax.ShapeDtypeStruct((1, FRAMES), F32),
             jax.ShapeDtypeStruct((1, FRAMES, 512), F32),
-            jax.ShapeDtypeStruct((1, 768), F32),
-            jax.ShapeDtypeStruct((5, 128), F32),
-            jax.ShapeDtypeStruct((10, 256), F32),
-            jax.ShapeDtypeStruct((20, 256), F32),
-            jax.ShapeDtypeStruct((1, 128), F32),
+            jax.ShapeDtypeStruct((2, TROWS + RROWS, 128), F32),
         ),
-        in_specs=[vmem] * 8,
-        out_specs=(vmem,) * 7,
+        in_specs=[pl.BlockSpec(memory_space=pltpu.HBM)] * 8,
+        out_specs=(vmem,) * 3,
         scratch_shapes=[
+            pltpu.VMEM((FRAMES, 512), BF16),
+            pltpu.VMEM((1, FRAMES), F32),
+            pltpu.VMEM((512, 768), BF16),
+            pltpu.VMEM((C0, 768), BF16),
+            pltpu.VMEM((HK * C0, C1), BF16),
+            pltpu.VMEM((HK * C1, C2), BF16),
+            pltpu.VMEM((HK * C2, C2), BF16),
+            pltpu.VMEM((6, 128), BF16),
+            dma((8,)),
             pltpu.VMEM((2, HALO, 512), BF16),
             pltpu.VMEM((2, 1, FRAMES), F32),
-            pltpu.VMEM((ROWS, 512), BF16),
             pltpu.VMEM((ROWS, HK * C1), BF16),
             pltpu.VMEM((ROWS, HK * C2), BF16),
             pltpu.VMEM((24, 2 * FRAMES), F32),
@@ -364,10 +388,23 @@
             dma((NZ - 1,)), dma((NZ - 1,)),
             dma, dma,
         ],
-        compiler_params=pltpu.CompilerParams(collective_id=0, has_side_effects=True),
-    )(features, cotangent, wp, ws, w1, w2, w3, wf.reshape(PK, C2))
-    scores, fgrad, sq, g1, g2, g3, gf = outs
-    return scores, fgrad, sq, g1, g2, g3, gf[0, : (PK * C2) // SHARES]
+        compiler_params=pltpu.CompilerParams(collective_id=0, has_side_effects=True, vmem_limit_bytes=24 << 20),
+    )(*(pltpu.with_memory_space_constraint(v, pltpu.HBM) for v in operands))
+    return pl.pallas_call(
+        finish,
+        out_shape=(
+            jax.ShapeDtypeStruct((1, FRAMES), F32),
+            jax.ShapeDtypeStruct((1, FRAMES, 512), F32),
+            jax.ShapeDtypeStruct((1, 768), F32),
+            jax.ShapeDtypeStruct((5, 128), F32),
+            jax.ShapeDtypeStruct((10, 256), F32),
+            jax.ShapeDtypeStruct((20, 256), F32),
+            jax.ShapeDtypeStruct(((PK * C2) // SHARES,), F32),
+        ),
+        in_specs=[vmem] * 3,
+        out_specs=(vmem,) * 7,
+        compiler_params=pltpu.CompilerParams(vmem_limit_bytes=4 << 20),
+    )(*outs)
 
 
 def solution(mesh):

time: 53.7 us -> 45.2 us (0.84)
  local copies, waits for them, and re-layouts: 7.2 us -> 0 us
  Pallas kernels: 45.1 us -> 43.9 us
    unnamed x18 -> x0, local copies, waits for them, and re-layouts: 5.42 us -> none
    pallas_call x1, Pallas kernels: 45.1 us -> 43.1 us  [shards(): pl.pallas_call(kernel, out_shape=(jax.ShapeDtypeStruct((1, FRAMES), F32),...]
    reshape x1 -> x0, local copies, waits for them, and re-layouts: 1.27 us -> none  [shards(): wf.reshape(PK, C2)]
    pallas_call x0 -> x1, Pallas kernels: none -> 0.74 us  [shards(): pl.pallas_call(finish, out_shape=(jax.ShapeDtypeStruct((1, FRAMES), F32),...]
where the time goes in v2:
time: 45.2 us; the launch traced here: 44.5 us
  Pallas kernels  43.9 us (97%)
  between operations  0.64 us (1%)
    pallas_call x1, Pallas kernels, shards(): pl.pallas_call(kernel, out_shape=(jax.ShapeDtypeStruct((1, FRAMES), F32),...  43.1 us

profile of v2, /device:TPU:1, one launch (start us, length us, event | category | flops | bytes accessed | tf_op | source)
XLA Modules:
  0.0 44.5 jit_solution(11325570278161167274)
XLA Ops:
  0.6 43.1 %shard_map.135 = (f32[1,128]{1,0:T(1,128)S(1)}, f32[1,128,512]{2,1,0:T(8,128)S(1)}, f32[2,40,128]{2,1,0:T(8,128)S(1)}) custom-call(bf16[1,128,512]{2,1,0:T(8,128)(2,1)} %feat_in.1, f32[1,128]{1,0:T(1,128)} %cot_in.1, bf16[512,768]{1,0:T(8,128)(2,1)} %wp_in.1, bf16[64,768]{1,0:T(8,128)(2,1)} %ws_in.1, bf16[320,128]{1,0:T(8,128)(2,1)} %w1_in.1, ...), custom_call_target="tpu_custom_call" | custom-call | tf_op jit(solution)/shard_map/pallas_call | solution.py:337
  43.8 0.7 %shard_map.136 = (f32[1,128]{1,0:T(1,128)}, f32[1,128,512]{2,1,0:T(8,128)}, f32[1,768]{1,0:T(1,128)}, f32[5,128]{1,0:T(8,128)}, f32[10,256]{1,0:T(8,128)}, /*index=5*/f32[20,256]{1,0:T(8,128)}, f32[12]{0:T(128)}) custom-call(f32[1,128]{1,0:T(1,128)S(1)} %get-tuple-element.10.scores_in, f32[1,128,512]{2,1,0:T(8,128)S(1)} %get-tuple-element.11.fgrad_in, ...), custom_call_target="tpu_custom_call" | custom-call | tf_op jit(solution)/shard_map/pallas_call | solution.py:393

commit v3 on v2

v3 whole, which is shorter than its diff:
```python
import math

import jax
import jax.numpy as jnp
from jax import lax
from jax.experimental import pallas as pl
from jax.experimental.pallas import tpu as pltpu
from jax.sharding import PartitionSpec as P

MESH = pl.DeviceIdType.MESH
F32 = jnp.float32
BF16 = jnp.bfloat16

C0, C1, C2 = 64, 128, 256
HK, PK = 5, 3
EPSILON = 1e-05
SLOPE = 0.1
FRAMES = 128
HALO = 16
ROWS = FRAMES + 2 * HALO
OWN = slice(HALO, HALO + FRAMES)

ZH, CORES, ZL, NX, NY = 4, 2, 2, 4, 8
NZ = ZH * ZL
SHARES = ZL * NX * NY
AR, CR, BR = 20, 10, 6


def dot(a, b, ca=1, cb=0):
    return lax.dot_general(a, b, (((ca,), (cb,)), ((), ())), preferred_element_type=F32)


def normalize(values):
    average = jnp.mean(values, axis=-1, keepdims=True)
    centred = values - average
    variance = jnp.mean(centred * centred, axis=-1, keepdims=True)
    inverse = lax.rsqrt(variance + EPSILON)
    return centred * inverse, inverse


def normalize_back(upstream, normed, inverse):
    first_mean = jnp.mean(upstream, axis=-1, keepdims=True)
    second_mean = jnp.mean(upstream * normed, axis=-1, keepdims=True)
    return (upstream - first_mean - normed * second_mean) * inverse


def activation(v):
    cumulative = 0.5 * (1.0 + lax.erf(v * math.sqrt(0.5)))
    density = jnp.exp(-0.5 * v * v) * (1.0 / math.sqrt(2.0 * math.pi))
    value = SLOPE * v + (1.0 - SLOPE) * (v * cumulative)
    slope = SLOPE + (1.0 - SLOPE) * (cumulative + v * density)
    return value, slope


def shifted(v, shift):
    return pltpu.roll(v, (-shift) % v.shape[0], 0) if shift else v


def split3(v):
    hi = v.astype(BF16).astype(F32)
    mid = (v - hi).astype(BF16).astype(F32)
    return hi, mid, (v - hi - mid).astype(BF16).astype(F32)


def kernel(
    feat_in, cot_in, wp_in, ws_in, w1_in, w2_in, w3_in, wf_in,
    scores, fgrad, fin_out,
    feat, cot, wp, ws, w1, w2, w3, wf, in_sem,
    hfeat, hcot, x1, x2, x3, cots, wfs, g3s, g1s, ast, bst,
    ab, a0, a1, ax, a2, ay, cb, c0, c1, cz, c2, cx, cs, c3, cy, bb, b0, b1, by, bs, b2, bx,
    zf, zs, zr, fin,
    hs, hr, s0, q0, sax, qax, say, qay, scz, qcz, scx, qcx, scy, qcy, sby, qby, sbx, qbx, sz, qz, s4, q4, relay,
):
    dp, sq = lax.axis_index("dp"), lax.axis_index("seq")
    zh, core = dp // CORES, dp % CORES
    zl, px, py = sq // (NX * NY), (sq // NY) % NX, sq % NY
    pz = zh * ZL + zl
    count = SHARES

    def at(z=None, x=None, y=None, c=None):
        z = pz if z is None else z
        x = px if x is None else x
        y = py if y is None else y
        c = core if c is None else c
        return ((z // ZL) * CORES + c, (z % ZL) * NX * NY + x * NY + y)

    partner = at(c=1 - core)
    has_low, has_high = sq > 0, sq < count - 1
    before = (jnp.where(has_low, dp, partner[0]), jnp.where(has_low, sq - 1, sq))
    after = (jnp.where(has_high, dp, partner[0]), jnp.where(has_high, sq + 1, sq))
    slot_before, slot_after = jnp.where(has_low, 1, 0), jnp.where(has_high, 0, 1)
    x_up, x_down = at(x=(px + 1) % NX), at(x=(px + NX - 1) % NX)
    y_up, y_down = at(y=(py + 1) % NY), at(y=(py + NY - 1) % NY)
    z_up, z_down = at(z=(pz + 1) % NZ), at(z=(pz + NZ - 1) % NZ)
    peers = [before, after, partner, x_up, x_down, y_up, y_down, z_up, z_down]

    barrier = pltpu.get_barrier_semaphore()
    for peer in peers:
        pl.semaphore_signal(barrier, inc=1, device_id=peer, device_id_type=MESH)
    sources = (feat_in.at[0], cot_in, wp_in, ws_in, w1_in, w2_in, w3_in, wf_in)
    loads = [
        pltpu.make_async_copy(source, target, in_sem.at[i])
        for i, (source, target) in enumerate(zip(sources, (feat, cot, wp, ws, w1, w2, w3, wf)))
    ]
    for load in loads:
        load.start()
    pl.semaphore_wait(barrier, len(peers))

    def send(src, dst, ss, rs, peer):
        copy = pltpu.make_async_remote_copy(
            src_ref=src, dst_ref=dst, send_sem=ss, recv_sem=rs, device_id=peer, device_id_type=MESH
        )
        copy.start()
        return copy

    loads[0].wait()
    loads[1].wait()
    halo = [
        send(feat.at[pl.ds(FRAMES - HALO, HALO)], hfeat.at[slot_after], hs.at[0], hr.at[slot_after], after),
        send(feat.at[pl.ds(0, HALO)], hfeat.at[slot_before], hs.at[1], hr.at[slot_before], before),
        send(cot, hcot.at[slot_after], hs.at[2], hr.at[2 + slot_after], after),
        send(cot, hcot.at[slot_before], hs.at[3], hr.at[2 + slot_before], before),
    ]

    def tell(*signals):
        for i, peer in signals:
            pl.semaphore_signal(relay.at[i], inc=1, device_id=peer, device_id_type=MESH)

    def hear(*indices):
        for i in indices:
            pl.semaphore_wait(relay.at[i], 1)

    tell((0, x_up), (1, y_up), (2, y_down), (3, z_up), (4, z_down))

    def front(rounded):
        projected = dot(rounded, wp[...]).astype(BF16)
        normed, inverse = normalize(projected.astype(F32))
        rounded = normed.astype(BF16)
        return normed, inverse, rounded, dot(rounded, ws[...], 1, 1)

    def chain(v1, masked):
        taps = [shifted(v1, k - 2).astype(BF16) for k in range(HK)] + [jnp.zeros(v1.shape, BF16)]
        t1 = jnp.concatenate(taps, axis=1)
        v2, slope1 = activation(dot(t1[:, : HK * C0], w1[...]))
        v2 = masked(v2)
        t2 = jnp.concatenate([shifted(v2, k - 2).astype(BF16) for k in range(HK)], axis=1)
        v3, slope2 = activation(dot(t2, w2[...]))
        v3 = masked(v3)
        t3 = jnp.concatenate([shifted(v3, k - 2).astype(BF16) for k in range(HK)], axis=1)
        v4, slope3 = activation(dot(t3, w3[...]))
        return (t1, t2, t3), (slope1, slope2, slope3, masked(v4))

    normed_in, inverse_in = normalize(feat[...].astype(F32))
    loads[2].wait()
    loads[3].wait()
    hidden_normed, hidden_inverse, hidden, squeezed = front(normed_in.astype(BF16))
    v1, squeezed_slope = activation(squeezed)
    for i in (4, 5, 6, 7):
        loads[i].wait()
    own_taps, own_rows = chain(v1, lambda v: v)
    for target, value in zip((x1, x2, x3), own_taps):
        target[...] = value
    for copy in halo:
        copy.wait_send()
    for i in range(2):
        for source, target, sem in ((feat.at[pl.ds(0, HALO)], hfeat.at[i], i), (cot, hcot.at[i], 2 + i)):
            pltpu.make_async_remote_copy(
                src_ref=source,
                dst_ref=target,
                send_sem=hs.at[sem],
                recv_sem=hr.at[sem],
                device_id=after,
                device_id_type=MESH,
            ).wait_recv()
    hear(0, 1, 2, 3, 4)
    tell((5, y_up), (6, y_down), (7, z_up), (8, z_down))
    edge = jnp.concatenate(
        [
            jnp.where(has_low, hfeat[0].astype(F32), 0.0),
            jnp.where(has_high, hfeat[1].astype(F32), 0.0),
        ],
        axis=0,
    )
    edge = activation(front(normalize(edge)[0].astype(BF16))[3])[0]
    edge = jnp.concatenate([edge[:HALO], v1[:HALO], v1[FRAMES - HALO :], edge[HALO:]], axis=0)
    row = lax.broadcasted_iota(jnp.int32, (4 * HALO, 1), 0)
    inside = jnp.logical_and(row >= jnp.where(has_low, 0, HALO), row < jnp.where(has_high, 4 * HALO, 3 * HALO))
    edge_taps, edge_rows = chain(edge, lambda v: jnp.where(inside, v, 0.0))
    for target, value in zip((x1, x2, x3), edge_taps):
        target[0:8] = value[HALO : HALO + 8]
        target[FRAMES - 8 : FRAMES] = value[3 * HALO - 8 : 3 * HALO]
    slope1, slope2, slope3, v4 = (
        jnp.concatenate([strip[: HALO + 8], mid[8 : FRAMES - 8], strip[3 * HALO - 8 :]], axis=0)
        for strip, mid in zip(edge_rows, own_rows)
    )
    row = lax.broadcasted_iota(jnp.int32, (ROWS, 1), 0)
    first_row = jnp.where(has_low, 0, HALO)
    last_row = jnp.where(has_high, ROWS, HALO + FRAMES)
    inside_all = jnp.logical_and(row >= first_row, row < last_row)

    def masked(v):
        return jnp.where(inside_all, v, 0.0)

    final_taps = [shifted(v4, k - 1)[OWN].astype(BF16) for k in range(PK)]
    wrow = [
        jnp.concatenate([wf[2 * k : 2 * k + 1, :], wf[2 * k + 1 : 2 * k + 2, :]], axis=1) for k in range(PK)
    ]
    total = sum(dot(jnp.broadcast_to(wrow[k], (8, C2)), final_taps[k], 1, 1) for k in range(PK))
    scores[...] = total[0:1]

    low = jnp.where(has_low, hcot[0], 0.0)
    high = jnp.where(has_high, hcot[1], 0.0)
    line = jnp.concatenate([low, cot[...], high], axis=1)
    cots[...] = jnp.zeros_like(cots)
    wfs[...] = jnp.zeros_like(wfs)
    pieces = split3(line)
    for p in range(3):
        for k in range(PK):
            start = FRAMES - HALO - k + 1
            cots[3 * k + p : 3 * k + p + 1, :] = pltpu.roll(pieces[p], 3 * FRAMES - start, 1)[:, : 2 * FRAMES]
            wfs[3 * k + p : 3 * k + p + 1, :] = wrow[k].astype(F32)
        cots[16 + p : 17 + p, 0:FRAMES] = pieces[p][:, FRAMES : 2 * FRAMES]
    upstream = dot(cots[0:16].astype(BF16), wfs[...].astype(BF16), 0, 0)[:ROWS]
    own_cot = cots[16:24, 0:FRAMES].astype(BF16)
    final_grad = [
        jnp.sum(dot(own_cot, final_taps[k]), axis=0, keepdims=True) for k in range(PK)
    ]

    hear(5, 6, 7, 8)
    tell((9, y_up), (10, z_up))
    delta = masked(upstream * slope3).astype(BF16)
    grad = dot(x3[...], delta[OWN], 0, 0)
    g3s[0], g3s[1] = grad[:, :128], grad[:, 128:]
    plane = NX * NY
    for h in range(CORES):
        for a in range(ZL):
            for r in range(AR):
                ast.at[h][pl.ds(a * AR + r, plane, stride=ZL * AR), :] = g3s.at[h][
                    pl.ds(a * plane * AR + r, plane, stride=AR), :
                ]
        for x in range(NX):
            ab[h, x] = ast[h, x * NY * ZL * AR : (x + 1) * NY * ZL * AR].astype(BF16)
    core_a = send(ab.at[1 - core], a0, s0.at[0], q0.at[0], partner)

    def back(delta, weight, width):
        d = delta.astype(F32)
        return sum(
            dot(shifted(d, 2 - k).astype(BF16), weight[k * width : (k + 1) * width], 1, 1)
            for k in range(HK)
        )

    def back_narrow(delta, weight, width):
        wide = dot(delta, weight[...], 1, 1)
        return sum(shifted(wide[:, k * width : (k + 1) * width], 2 - k) for k in range(HK))

    upstream = back(delta, w3, C2)
    delta = masked(upstream * slope2).astype(BF16)
    grad = dot(x2[...], delta[OWN], 0, 0)
    for h in range(CORES):
        cb[h] = grad[:, h * 128 : (h + 1) * 128].astype(BF16).reshape(ZL, NX, NY * CR, 128)
    core_c = send(cb.at[1 - core], c0, s0.at[1], q0.at[1], partner)

    upstream = back_narrow(delta, w2, C1)
    delta = masked(upstream * slope1).astype(BF16)
    g1s[...] = dot(x1[...], delta[OWN], 0, 0)
    lines = [(a * plane + x * NY, (x * ZL + a) * BR) for a in range(ZL) for x in range(NX)]
    step = NX * ZL * BR
    for share, row in lines:
        for r in range(5):
            bst.at[1][pl.ds(row + r, NY, stride=step), :] = g1s[pl.ds(5 * share + r, NY, stride=5), :]

    flat = jnp.concatenate(final_grad, axis=1)
    width = (PK * C2) // SHARES
    offset = lax.broadcasted_iota(jnp.int32, (SHARES, PK * C2), 1) - width * lax.broadcasted_iota(
        jnp.int32, (SHARES, PK * C2), 0
    )
    picked = jnp.where(jnp.logical_and(offset >= 0, offset < width), flat, 0.0).astype(BF16)
    place = lax.broadcasted_iota(jnp.int32, (PK * C2, 128), 0)
    place = place - width * ((place * 5462) >> 16) - lax.broadcasted_iota(jnp.int32, (PK * C2, 128), 1)
    spread = jnp.where(place == 0, 1.0, 0.0).astype(BF16)
    spread = dot(picked, spread)
    for share, row in lines:
        bst.at[1][pl.ds(row + 5, NY, stride=step), :] = spread[share : share + NY]

    upstream = back_narrow(delta, w1, C0)
    delta_squeeze = (upstream[OWN] * squeezed_slope).astype(BF16)
    grad = dot(delta_squeeze, hidden, 0, 0)
    for share, row in lines:
        for j in range(BR):
            bst.at[0][pl.ds(row + j, NY, stride=step), :] = grad[share : share + NY, j * 128 : (j + 1) * 128]
    for h in range(CORES):
        for y in range(NY):
            bb[h, y] = bst[h, y * step : (y + 1) * step].astype(BF16)
    core_b = send(bb.at[1 - core], b0, s0.at[2], q0.at[2], partner)

    def along_x(source, target, ss, rs):
        return [
            send(source.at[(px + d) % NX], target.at[d - 1], ss.at[d - 1], rs.at[d - 1], at(x=(px + d) % NX))
            for d in range(1, NX)
        ]

    def along_y(source, target, ss, rs):
        return [
            send(source.at[(py + d) % NY], target.at[d - 1], ss.at[d - 1], rs.at[d - 1], at(y=(py + d) % NY))
            for d in range(1, NY)
        ]

    def gathered(copies, own, arrived):
        for copy in copies:
            copy.wait()
        acc = own.astype(F32)
        for d in range(len(copies)):
            acc = acc + arrived[d].astype(F32)
        return acc

    hear(9, 10)
    core_a.wait()
    a1[...] = (ab[core].astype(F32) + a0[...].astype(F32)).astype(BF16)
    a_x = along_x(a1, ax, sax, qax)
    core_c.wait()
    c1[...] = (cb[core].astype(F32) + c0[...].astype(F32)).astype(BF16)
    pair = pz + 1 - 2 * zl
    c_z = send(c1.at[1 - zl], cz, scz, qcz, at(z=pair))
    core_b.wait()
    b1[...] = (bb[core].astype(F32) + b0[...].astype(F32)).astype(BF16)
    b_y = along_y(b1, by, sby, qby)

    hidden_upstream = dot(delta_squeeze, ws[...])
    projected_grad = normalize_back(hidden_upstream, hidden_normed, hidden_inverse).astype(BF16)
    normed_grad = dot(projected_grad, wp[...], 1, 1)
    fgrad[0] = normalize_back(normed_grad, normed_in, inverse_in)

    c_z.wait()
    c2[...] = (c1[zl].astype(F32) + cz[...].astype(F32)).astype(BF16)
    c_x = along_x(c2, cx, scx, qcx)
    a2[...] = gathered(a_x, a1[px], ax).astype(BF16).reshape(NY, ZL * AR, 128)
    a_y = along_y(a2, ay, say, qay)
    bs[0:step] = gathered(b_y, b1[py], by)
    bs[step:] = jnp.zeros((8, 128), F32)
    for x in range(NX):
        b2[x] = bs[x * ZL * BR : x * ZL * BR + 16].astype(BF16)
    b_x = along_x(b2, bx, sbx, qbx)
    cs[0 : NY * CR] = gathered(c_x, c2[px], cx)
    cs[NY * CR :] = jnp.zeros((8, 128), F32)
    for y in range(NY):
        c3[y] = cs[y * CR : y * CR + 16].astype(BF16)
    c_y = along_y(c3, cy, scy, qcy)

    zf[...] = jnp.zeros_like(zf)
    total = gathered(b_x, b2[px], bx)
    for a in range(ZL):
        zf[a, AR : AR + BR] = total[a * BR : (a + 1) * BR]
    total = gathered(a_y, a2[py], ay)
    for a in range(ZL):
        zf[a, 0:AR] = total[a * AR : (a + 1) * AR]
    total = gathered(c_y, c3[py], cy)
    for a in range(ZL):
        zf[a, 32:48] = total
    zs[...] = zf[...].astype(BF16)

    along_z = []
    for d in range(1, NZ):
        target = (pz + d) % NZ
        rows = 32 if d % ZL else 48
        along_z.append(
            send(
                zs.at[target % ZL, pl.ds(0, rows)], zr.at[d, pl.ds(0, rows)], sz.at[d - 1], qz.at[d - 1], at(z=target)
            )
        )
    for copy in along_z:
        copy.wait()
    zr[0] = zs[zl]
    scale = 1.0 / math.sqrt(FRAMES * SHARES * ZH * CORES)
    acc = jnp.zeros((32, 128), F32)
    for z in range(NZ):
        acc = acc + zr[(pz + NZ - z) % NZ, 0:32].astype(F32)
    fin[core, 0:32] = acc * scale
    acc = jnp.zeros((16, 128), F32)
    for z in range(ZH):
        acc = acc + zr[(pz + NZ - (z * ZL + zl)) % NZ, 32:48].astype(F32)
    fin[core, 32:48] = acc * scale
    send(fin.at[core], fin.at[core], s4, q4, partner).wait()

    fin_out[...] = fin[...]


def finish(scores_in, fgrad_in, fin, scores, fgrad, sq_out, g1_out, g2_out, g3_out, gf_out):
    scores[...] = scores_in[...]
    fgrad[...] = fgrad_in[...]
    g3_out[...] = jnp.concatenate([fin[0, 0:20], fin[1, 0:20]], axis=1)
    g2_out[...] = jnp.concatenate([fin[0, 32:42], fin[1, 32:42]], axis=1)
    g1_out[...] = fin[1, 20:25]
    gf_out[...] = fin[1, 25:26].reshape(128)[: (PK * C2) // SHARES]
    for j in range(6):
        sq_out[:, j * 128 : (j + 1) * 128] = fin[0, 20 + j : 21 + j]


def shards(features, cotangent, wp, ws, w1, w2, w3, wf):
    vmem = pl.BlockSpec(memory_space=pltpu.VMEM)
    operands = (features, cotangent, wp, ws, w1, w2, w3, wf.reshape(6, 128))
    dma = pltpu.SemaphoreType.DMA
    outs = pl.pallas_call(
        kernel,
        out_shape=(
            jax.ShapeDtypeStruct((1, FRAMES), F32),
            jax.ShapeDtypeStruct((1, FRAMES, 512), F32),
            jax.ShapeDtypeStruct((2, 48, 128), F32),
        ),
        in_specs=[pl.BlockSpec(memory_space=pltpu.HBM)] * 8,
        out_specs=(vmem,) * 3,
        scratch_shapes=[
            pltpu.VMEM((FRAMES, 512), BF16),
            pltpu.VMEM((1, FRAMES), F32),
            pltpu.VMEM((512, 768), BF16),
            pltpu.VMEM((C0, 768), BF16),
            pltpu.VMEM((HK * C0, C1), BF16),
            pltpu.VMEM((HK * C1, C2), BF16),
            pltpu.VMEM((HK * C2, C2), BF16),
            pltpu.VMEM((6, 128), BF16),
            dma((8,)),
            pltpu.VMEM((2, HALO, 512), BF16),
            pltpu.VMEM((2, 1, FRAMES), F32),
            pltpu.VMEM((FRAMES, (HK + 1) * C0), BF16),
            pltpu.VMEM((FRAMES, HK * C1), BF16),
            pltpu.VMEM((FRAMES, HK * C2), BF16),
            pltpu.VMEM((24, 2 * FRAMES), F32),
            pltpu.VMEM((16, C2), F32),
            pltpu.VMEM((2, HK * C2, 128), F32),
            pltpu.VMEM(((HK + 1) * C0, 128), F32),
            pltpu.VMEM((2, SHARES * AR, 128), F32),
            pltpu.VMEM((2, SHARES * BR, 128), F32),
            pltpu.VMEM((2, NX, NY * ZL * AR, 128), BF16),
            pltpu.VMEM((NX, NY * ZL * AR, 128), BF16),
            pltpu.VMEM((NX, NY * ZL * AR, 128), BF16),
            pltpu.VMEM((NX - 1, NY * ZL * AR, 128), BF16),
            pltpu.VMEM((NY, ZL * AR, 128), BF16),
            pltpu.VMEM((NY - 1, ZL * AR, 128), BF16),
            pltpu.VMEM((2, ZL, NX, NY * CR, 128), BF16),
            pltpu.VMEM((ZL, NX, NY * CR, 128), BF16),
            pltpu.VMEM((ZL, NX, NY * CR, 128), BF16),
            pltpu.VMEM((NX, NY * CR, 128), BF16),
            pltpu.VMEM((NX, NY * CR, 128), BF16),
            pltpu.VMEM((NX - 1, NY * CR, 128), BF16),
            pltpu.VMEM((NY * CR + 8, 128), F32),
            pltpu.VMEM((NY, 16, 128), BF16),
            pltpu.VMEM((NY - 1, 16, 128), BF16),
            pltpu.VMEM((2, NY, NX * ZL * BR, 128), BF16),
            pltpu.VMEM((NY, NX * ZL * BR, 128), BF16),
            pltpu.VMEM((NY, NX * ZL * BR, 128), BF16),
            pltpu.VMEM((NY - 1, NX * ZL * BR, 128), BF16),
            pltpu.VMEM((NX * ZL * BR + 8, 128), F32),
            pltpu.VMEM((NX, 16, 128), BF16),
            pltpu.VMEM((NX - 1, 16, 128), BF16),
            pltpu.VMEM((ZL, 48, 128), F32),
            pltpu.VMEM((ZL, 48, 128), BF16),
            pltpu.VMEM((NZ, 48, 128), BF16),
            pltpu.VMEM((2, 48, 128), F32),
            dma((4,)), dma((4,)),
            dma((3,)), dma((3,)),
            dma((NX - 1,)), dma((NX - 1,)),
            dma((NY - 1,)), dma((NY - 1,)),
            dma, dma,
            dma((NX - 1,)), dma((NX - 1,)),
            dma((NY - 1,)), dma((NY - 1,)),
            dma((NY - 1,)), dma((NY - 1,)),
            dma((NX - 1,)), dma((NX - 1,)),
            dma((NZ - 1,)), dma((NZ - 1,)),
            dma, dma,
            pltpu.SemaphoreType.REGULAR((11,)),
        ],
        compiler_params=pltpu.CompilerParams(collective_id=0, has_side_effects=True, vmem_limit_bytes=24 << 20),
    )(*(pltpu.with_memory_space_constraint(v, pltpu.HBM) for v in operands))
    return pl.pallas_call(
        finish,
        out_shape=(
            jax.ShapeDtypeStruct((1, FRAMES), F32),
            jax.ShapeDtypeStruct((1, FRAMES, 512), F32),
            jax.ShapeDtypeStruct((1, 768), F32),
            jax.ShapeDtypeStruct((5, 128), F32),
            jax.ShapeDtypeStruct((10, 256), F32),
            jax.ShapeDtypeStruct((20, 256), F32),
            jax.ShapeDtypeStruct(((PK * C2) // SHARES,), F32),
        ),
        in_specs=[vmem] * 3,
        out_specs=(vmem,) * 7,
        compiler_params=pltpu.CompilerParams(vmem_limit_bytes=4 << 20),
    )(*outs)


def solution(mesh):
    placed = (P("dp", "seq", None), P("dp", "seq"), P(), P(), P(), P(), P(), P())
    return jax.shard_map(
        shards,
        mesh=mesh,
        in_specs=placed,
        out_specs=(
            P("dp", "seq"),
            P("dp", "seq", None),
            P("seq", None),
            P("seq", None),
            P("seq", None),
            P("seq", None),
            P("seq"),
        ),
        check_vma=False,
    )
```

time: 45.2 us -> 43 us (0.951); the launches traced: 44.5 us -> 42.9 us
  Pallas kernels: 43.9 us -> 42.3 us
    pallas_call x1, Pallas kernels: 43.1 us -> 41.5 us  [shards(): pl.pallas_call(kernel, out_shape=(jax.ShapeDtypeStruct((1, FRAMES), F32),...]
where the time goes in v3:
time: 43 us; the launch traced here: 42.9 us
  Pallas kernels  42.3 us (98%)
  between operations  0.64 us (1%)
    pallas_call x1, Pallas kernels, shards(): pl.pallas_call(kernel, out_shape=(jax.ShapeDtypeStruct((1, FRAMES), F32),...  41.5 us

profile of v3, /device:TPU:1, one launch (start us, length us, event | category | flops | bytes accessed | tf_op | source)
XLA Modules:
  0.0 42.9 jit_solution(202006990718480721)
XLA Ops:
  0.6 41.5 %shard_map.135 = (f32[1,128]{1,0:T(1,128)S(1)}, f32[1,128,512]{2,1,0:T(8,128)S(1)}, f32[2,48,128]{2,1,0:T(8,128)S(1)}) custom-call(bf16[1,128,512]{2,1,0:T(8,128)(2,1)} %feat_in.1, f32[1,128]{1,0:T(1,128)} %cot_in.1, bf16[512,768]{1,0:T(8,128)(2,1)} %wp_in.1, bf16[64,768]{1,0:T(8,128)(2,1)} %ws_in.1, bf16[320,128]{1,0:T(8,128)(2,1)} %w1_in.1, ...), custom_call_target="tpu_custom_call" | custom-call | tf_op jit(solution)/shard_map/pallas_call | solution.py:402
  42.2 0.7 %shard_map.136 = (f32[1,128]{1,0:T(1,128)}, f32[1,128,512]{2,1,0:T(8,128)}, f32[1,768]{1,0:T(1,128)}, f32[5,128]{1,0:T(8,128)}, f32[10,256]{1,0:T(8,128)}, /*index=5*/f32[20,256]{1,0:T(8,128)}, f32[12]{0:T(128)}) custom-call(f32[1,128]{1,0:T(1,128)S(1)} %get-tuple-element.10.scores_in, f32[1,128,512]{2,1,0:T(8,128)S(1)} %get-tuple-element.11.fgrad_in, ...), custom_call_target="tpu_custom_call" | custom-call | tf_op jit(solution)/shard_map/pallas_call | solution.py:473

commit v4 on v3

--- a/solution.py
+++ b/solution.py
@@ -23,7 +23,8 @@
 ZH, CORES, ZL, NX, NY = 4, 2, 2, 4, 8
 NZ = ZH * ZL
 SHARES = ZL * NX * NY
-AR, CR, BR = 20, 10, 6
+AR, CR, BR = 20, 8, 8
+SECOND = 10
 
 
 def dot(a, b, ca=1, cb=0):
@@ -66,10 +67,10 @@
     feat_in, cot_in, wp_in, ws_in, w1_in, w2_in, w3_in, wf_in,
     scores, fgrad, fin_out,
     feat, cot, wp, ws, w1, w2, w3, wf, in_sem,
-    hfeat, hcot, x1, x2, x3, cots, wfs, g3s, g1s, ast, bst,
-    ab, a0, a1, ax, a2, ay, cb, c0, c1, cz, c2, cx, cs, c3, cy, bb, b0, b1, by, bs, b2, bx,
-    zf, zs, zr, fin,
-    hs, hr, s0, q0, sax, qax, say, qay, scz, qcz, scx, qcx, scy, qcy, sby, qby, sbx, qbx, sz, qz, s4, q4, relay,
+    hfeat, hcot, x1, x2, x3, cots, wfs, g3s, g2s, g1s, ast, cst, bst,
+    ab, a0, a1, ax, a2, ay, cb, c0, c1, cz, c2, cx, c3, cy, bb, b0, b1, by, b2, bx,
+    zf, zs, zr, zc, fin,
+    hs, hr, s0, q0, sax, qax, say, qay, scz, qcz, scx, qcx, scy, qcy, sby, qby, sbx, qbx, sz, qz, szc, qzc, s4, q4, relay,
 ):
     dp, sq = lax.axis_index("dp"), lax.axis_index("seq")
     zh, core = dp // CORES, dp % CORES
@@ -111,7 +112,10 @@
             src_ref=src, dst_ref=dst, send_sem=ss, recv_sem=rs, device_id=peer, device_id_type=MESH
         )
         copy.start()
+        sent.append(copy)
         return copy
+
+    sent = []
 
     loads[0].wait()
     loads[1].wait()
@@ -160,8 +164,6 @@
     own_taps, own_rows = chain(v1, lambda v: v)
     for target, value in zip((x1, x2, x3), own_taps):
         target[...] = value
-    for copy in halo:
-        copy.wait_send()
     for i in range(2):
         for source, target, sem in ((feat.at[pl.ds(0, HALO)], hfeat.at[i], i), (cot, hcot.at[i], 2 + i)):
             pltpu.make_async_remote_copy(
@@ -201,13 +203,9 @@
     def masked(v):
         return jnp.where(inside_all, v, 0.0)
 
-    final_taps = [shifted(v4, k - 1)[OWN].astype(BF16) for k in range(PK)]
     wrow = [
         jnp.concatenate([wf[2 * k : 2 * k + 1, :], wf[2 * k + 1 : 2 * k + 2, :]], axis=1) for k in range(PK)
     ]
-    total = sum(dot(jnp.broadcast_to(wrow[k], (8, C2)), final_taps[k], 1, 1) for k in range(PK))
-    scores[...] = total[0:1]
-
     low = jnp.where(has_low, hcot[0], 0.0)
     high = jnp.where(has_high, hcot[1], 0.0)
     line = jnp.concatenate([low, cot[...], high], axis=1)
@@ -221,11 +219,6 @@
             wfs[3 * k + p : 3 * k + p + 1, :] = wrow[k].astype(F32)
         cots[16 + p : 17 + p, 0:FRAMES] = pieces[p][:, FRAMES : 2 * FRAMES]
     upstream = dot(cots[0:16].astype(BF16), wfs[...].astype(BF16), 0, 0)[:ROWS]
-    own_cot = cots[16:24, 0:FRAMES].astype(BF16)
-    final_grad = [
-        jnp.sum(dot(own_cot, final_taps[k]), axis=0, keepdims=True) for k in range(PK)
-    ]
-
     hear(5, 6, 7, 8)
     tell((9, y_up), (10, z_up))
     delta = masked(upstream * slope3).astype(BF16)
@@ -257,14 +250,33 @@
     delta = masked(upstream * slope2).astype(BF16)
     grad = dot(x2[...], delta[OWN], 0, 0)
     for h in range(CORES):
-        cb[h] = grad[:, h * 128 : (h + 1) * 128].astype(BF16).reshape(ZL, NX, NY * CR, 128)
+        g2s[h] = grad[:, h * 128 : (h + 1) * 128]
+        for r in range(CR):
+            cst.at[h][pl.ds(r, SHARES, stride=CR), :] = g2s.at[h][pl.ds(r, SHARES, stride=SECOND), :]
+        cb[h] = cst[h].astype(BF16).reshape(ZL, NX, NY * CR, 128)
     core_c = send(cb.at[1 - core], c0, s0.at[1], q0.at[1], partner)
+
+    final_taps = [shifted(v4, k - 1)[OWN].astype(BF16) for k in range(PK)]
+    total = sum(dot(jnp.broadcast_to(wrow[k], (8, C2)), final_taps[k], 1, 1) for k in range(PK))
+    scores[...] = total[0:1]
+
+
+    own_cot = cots[16:24, 0:FRAMES].astype(BF16)
+    final_grad = [
+        jnp.sum(dot(own_cot, final_taps[k]), axis=0, keepdims=True) for k in range(PK)
+    ]
 
     upstream = back_narrow(delta, w2, C1)
     delta = masked(upstream * slope1).astype(BF16)
     g1s[...] = dot(x1[...], delta[OWN], 0, 0)
     lines = [(a * plane + x * NY, (x * ZL + a) * BR) for a in range(ZL) for x in range(NX)]
     step = NX * ZL * BR
+    for h in range(CORES):
+        for share, row in lines:
+            for r in range(CR, SECOND):
+                bst.at[h][pl.ds(row + r - 2, NY, stride=step), :] = g2s.at[h][
+                    pl.ds(SECOND * share + r, NY, stride=SECOND), :
+                ]
     for share, row in lines:
         for r in range(5):
             bst.at[1][pl.ds(row + r, NY, stride=step), :] = g1s[pl.ds(5 * share + r, NY, stride=5), :]
@@ -286,7 +298,7 @@
     delta_squeeze = (upstream[OWN] * squeezed_slope).astype(BF16)
     grad = dot(delta_squeeze, hidden, 0, 0)
     for share, row in lines:
-        for j in range(BR):
+        for j in range(6):
             bst.at[0][pl.ds(row + j, NY, stride=step), :] = grad[share : share + NY, j * 128 : (j + 1) * 128]
     for h in range(CORES):
         for y in range(NY):
@@ -307,21 +319,21 @@
 
     def gathered(copies, own, arrived):
         for copy in copies:
-            copy.wait()
+            copy.wait_recv()
         acc = own.astype(F32)
         for d in range(len(copies)):
             acc = acc + arrived[d].astype(F32)
         return acc
 
     hear(9, 10)
-    core_a.wait()
+    core_a.wait_recv()
     a1[...] = (ab[core].astype(F32) + a0[...].astype(F32)).astype(BF16)
     a_x = along_x(a1, ax, sax, qax)
-    core_c.wait()
+    core_c.wait_recv()
     c1[...] = (cb[core].astype(F32) + c0[...].astype(F32)).astype(BF16)
     pair = pz + 1 - 2 * zl
     c_z = send(c1.at[1 - zl], cz, scz, qcz, at(z=pair))
-    core_b.wait()
+    core_b.wait_recv()
     b1[...] = (bb[core].astype(F32) + b0[...].astype(F32)).astype(BF16)
     b_y = along_y(b1, by, sby, qby)
 
@@ -330,20 +342,14 @@
     normed_grad = dot(projected_grad, wp[...], 1, 1)
     fgrad[0] = normalize_back(normed_grad, normed_in, inverse_in)
 
-    c_z.wait()
+    c_z.wait_recv()
     c2[...] = (c1[zl].astype(F32) + cz[...].astype(F32)).astype(BF16)
     c_x = along_x(c2, cx, scx, qcx)
     a2[...] = gathered(a_x, a1[px], ax).astype(BF16).reshape(NY, ZL * AR, 128)
     a_y = along_y(a2, ay, say, qay)
-    bs[0:step] = gathered(b_y, b1[py], by)
-    bs[step:] = jnp.zeros((8, 128), F32)
-    for x in range(NX):
-        b2[x] = bs[x * ZL * BR : x * ZL * BR + 16].astype(BF16)
+    b2[...] = gathered(b_y, b1[py], by).astype(BF16).reshape(NX, ZL * BR, 128)
     b_x = along_x(b2, bx, sbx, qbx)
-    cs[0 : NY * CR] = gathered(c_x, c2[px], cx)
-    cs[NY * CR :] = jnp.zeros((8, 128), F32)
-    for y in range(NY):
-        c3[y] = cs[y * CR : y * CR + 16].astype(BF16)
+    c3[...] = gathered(c_x, c2[px], cx).astype(BF16).reshape(NY, CR, 128)
     c_y = along_y(c3, cy, scy, qcy)
 
     zf[...] = jnp.zeros_like(zf)
@@ -353,42 +359,42 @@
     total = gathered(a_y, a2[py], ay)
     for a in range(ZL):
         zf[a, 0:AR] = total[a * AR : (a + 1) * AR]
-    total = gathered(c_y, c3[py], cy)
-    for a in range(ZL):
-        zf[a, 32:48] = total
     zs[...] = zf[...].astype(BF16)
-
     along_z = []
     for d in range(1, NZ):
         target = (pz + d) % NZ
-        rows = 32 if d % ZL else 48
+        along_z.append(send(zs.at[target % ZL], zr.at[d], sz.at[d - 1], qz.at[d - 1], at(z=target)))
+    zc[0] = gathered(c_y, c3[py], cy).astype(BF16)
+    for d in range(1, ZH):
         along_z.append(
-            send(
-                zs.at[target % ZL, pl.ds(0, rows)], zr.at[d, pl.ds(0, rows)], sz.at[d - 1], qz.at[d - 1], at(z=target)
-            )
+            send(zc.at[0], zc.at[d], szc.at[d - 1], qzc.at[d - 1], at(z=(pz + ZL * d) % NZ))
         )
     for copy in along_z:
-        copy.wait()
+        copy.wait_recv()
     zr[0] = zs[zl]
     scale = 1.0 / math.sqrt(FRAMES * SHARES * ZH * CORES)
     acc = jnp.zeros((32, 128), F32)
     for z in range(NZ):
-        acc = acc + zr[(pz + NZ - z) % NZ, 0:32].astype(F32)
+        acc = acc + zr[(pz + NZ - z) % NZ].astype(F32)
     fin[core, 0:32] = acc * scale
-    acc = jnp.zeros((16, 128), F32)
+    acc = jnp.zeros((CR, 128), F32)
     for z in range(ZH):
-        acc = acc + zr[(pz + NZ - (z * ZL + zl)) % NZ, 32:48].astype(F32)
-    fin[core, 32:48] = acc * scale
-    send(fin.at[core], fin.at[core], s4, q4, partner).wait()
+        acc = acc + zc[(zh + ZH - z) % ZH].astype(F32)
+    fin[core, 32:40] = acc * scale
+    send(fin.at[core], fin.at[core], s4, q4, partner).wait_recv()
 
     fin_out[...] = fin[...]
+    for copy in sent:
+        copy.wait_send()
 
 
 def finish(scores_in, fgrad_in, fin, scores, fgrad, sq_out, g1_out, g2_out, g3_out, gf_out):
     scores[...] = scores_in[...]
     fgrad[...] = fgrad_in[...]
     g3_out[...] = jnp.concatenate([fin[0, 0:20], fin[1, 0:20]], axis=1)
-    g2_out[...] = jnp.concatenate([fin[0, 32:42], fin[1, 32:42]], axis=1)
+    for h in range(CORES):
+        g2_out[0:CR, h * 128 : (h + 1) * 128] = fin[h, 32:40]
+        g2_out[CR:SECOND, h * 128 : (h + 1) * 128] = fin[h, 26:28]
     g1_out[...] = fin[1, 20:25]
     gf_out[...] = fin[1, 25:26].reshape(128)[: (PK * C2) // SHARES]
     for j in range(6):
@@ -404,7 +410,7 @@
         out_shape=(
             jax.ShapeDtypeStruct((1, FRAMES), F32),
             jax.ShapeDtypeStruct((1, FRAMES, 512), F32),
-            jax.ShapeDtypeStruct((2, 48, 128), F32),
+            jax.ShapeDtypeStruct((2, 40, 128), F32),
         ),
         in_specs=[pl.BlockSpec(memory_space=pltpu.HBM)] * 8,
         out_specs=(vmem,) * 3,
@@ -426,8 +432,10 @@
             pltpu.VMEM((24, 2 * FRAMES), F32),
             pltpu.VMEM((16, C2), F32),
             pltpu.VMEM((2, HK * C2, 128), F32),
+            pltpu.VMEM((2, HK * C1, 128), F32),
             pltpu.VMEM(((HK + 1) * C0, 128), F32),
             pltpu.VMEM((2, SHARES * AR, 128), F32),
+            pltpu.VMEM((2, SHARES * CR, 128), F32),
             pltpu.VMEM((2, SHARES * BR, 128), F32),
             pltpu.VMEM((2, NX, NY * ZL * AR, 128), BF16),
             pltpu.VMEM((NX, NY * ZL * AR, 128), BF16),
@@ -441,20 +449,19 @@
             pltpu.VMEM((NX, NY * CR, 128), BF16),
             pltpu.VMEM((NX, NY * CR, 128), BF16),
             pltpu.VMEM((NX - 1, NY * CR, 128), BF16),
-            pltpu.VMEM((NY * CR + 8, 128), F32),
-            pltpu.VMEM((NY, 16, 128), BF16),
-            pltpu.VMEM((NY - 1, 16, 128), BF16),
+            pltpu.VMEM((NY, CR, 128), BF16),
+            pltpu.VMEM((NY - 1, CR, 128), BF16),
             pltpu.VMEM((2, NY, NX * ZL * BR, 128), BF16),
             pltpu.VMEM((NY, NX * ZL * BR, 128), BF16),
             pltpu.VMEM((NY, NX * ZL * BR, 128), BF16),
             pltpu.VMEM((NY - 1, NX * ZL * BR, 128), BF16),
-            pltpu.VMEM((NX * ZL * BR + 8, 128), F32),
-            pltpu.VMEM((NX, 16, 128), BF16),
-            pltpu.VMEM((NX - 1, 16, 128), BF16),
-            pltpu.VMEM((ZL, 48, 128), F32),
-            pltpu.VMEM((ZL, 48, 128), BF16),
-            pltpu.VMEM((NZ, 48, 128), BF16),
-            pltpu.VMEM((2, 48, 128), F32),
+            pltpu.VMEM((NX, ZL * BR, 128), BF16),
+            pltpu.VMEM((NX - 1, ZL * BR, 128), BF16),
+            pltpu.VMEM((ZL, 32, 128), F32),
+            pltpu.VMEM((ZL, 32, 128), BF16),
+            pltpu.VMEM((NZ, 32, 128), BF16),
+            pltpu.VMEM((ZH, CR, 128), BF16),
+            pltpu.VMEM((2, 40, 128), F32),
             dma((4,)), dma((4,)),
             dma((3,)), dma((3,)),
             dma((NX - 1,)), dma((NX - 1,)),
@@ -465,6 +472,7 @@
             dma((NY - 1,)), dma((NY - 1,)),
             dma((NX - 1,)), dma((NX - 1,)),
             dma((NZ - 1,)), dma((NZ - 1,)),
+            dma((ZH - 1,)), dma((ZH - 1,)),
             dma, dma,
             pltpu.SemaphoreType.REGULAR((11,)),
         ],

time: 43 us -> 41.8 us (0.972)
  Pallas kernels: 42.3 us -> 41.1 us
    pallas_call x1, Pallas kernels: 41.5 us -> 40.3 us  [shards(): pl.pallas_call(kernel, out_shape=(jax.ShapeDtypeStruct((1, FRAMES), F32),...]
where the time goes in v4:
time: 41.8 us; the launch traced here: 41.7 us
  Pallas kernels  41.1 us (98%)
  between operations  0.64 us (2%)
    pallas_call x1, Pallas kernels, shards(): pl.pallas_call(kernel, out_shape=(jax.ShapeDtypeStruct((1, FRAMES), F32),...  40.3 us

profile of v4, /device:TPU:1, one launch (start us, length us, event | category | flops | bytes accessed | tf_op | source)
XLA Modules:
  0.0 41.7 jit_solution(17849216571655258528)
XLA Ops:
  0.6 40.3 %shard_map.135 = (f32[1,128]{1,0:T(1,128)S(1)}, f32[1,128,512]{2,1,0:T(8,128)S(1)}, f32[2,40,128]{2,1,0:T(8,128)S(1)}) custom-call(bf16[1,128,512]{2,1,0:T(8,128)(2,1)} %feat_in.1, f32[1,128]{1,0:T(1,128)} %cot_in.1, bf16[512,768]{1,0:T(8,128)(2,1)} %wp_in.1, bf16[64,768]{1,0:T(8,128)(2,1)} %ws_in.1, bf16[320,128]{1,0:T(8,128)(2,1)} %w1_in.1, ...), custom_call_target="tpu_custom_call" | custom-call | tf_op jit(solution)/shard_map/pallas_call | solution.py:408
  41.0 0.7 %shard_map.136 = (f32[1,128]{1,0:T(1,128)}, f32[1,128,512]{2,1,0:T(8,128)}, f32[1,768]{1,0:T(1,128)}, f32[5,128]{1,0:T(8,128)}, f32[10,256]{1,0:T(8,128)}, /*index=5*/f32[20,256]{1,0:T(8,128)}, f32[12]{0:T(128)}) custom-call(f32[1,128]{1,0:T(1,128)S(1)} %get-tuple-element.10.scores_in, f32[1,128,512]{2,1,0:T(8,128)S(1)} %get-tuple-element.11.fgrad_in, ...), custom_call_target="tpu_custom_call" | custom-call | tf_op jit(solution)/shard_map/pallas_call | solution.py:481

commit v5 on v4

--- a/solution.py
+++ b/solution.py
@@ -176,6 +176,22 @@
             ).wait_recv()
     hear(0, 1, 2, 3, 4)
     tell((5, y_up), (6, y_down), (7, z_up), (8, z_down))
+    wrow = [
+        jnp.concatenate([wf[2 * k : 2 * k + 1, :], wf[2 * k + 1 : 2 * k + 2, :]], axis=1) for k in range(PK)
+    ]
+    low = jnp.where(has_low, hcot[0], 0.0)
+    high = jnp.where(has_high, hcot[1], 0.0)
+    line = jnp.concatenate([low, cot[...], high], axis=1)
+    cots[...] = jnp.zeros_like(cots)
+    wfs[...] = jnp.zeros_like(wfs)
+    pieces = split3(line)
+    for p in range(3):
+        for k in range(PK):
+            start = FRAMES - HALO - k + 1
+            cots[3 * k + p : 3 * k + p + 1, :] = pltpu.roll(pieces[p], 3 * FRAMES - start, 1)[:, : 2 * FRAMES]
+            wfs[3 * k + p : 3 * k + p + 1, :] = wrow[k].astype(F32)
+        cots[16 + p : 17 + p, 0:FRAMES] = pieces[p][:, FRAMES : 2 * FRAMES]
+    upstream = dot(cots[0:16].astype(BF16), wfs[...].astype(BF16), 0, 0)[:ROWS]
     edge = jnp.concatenate(
         [
             jnp.where(has_low, hfeat[0].astype(F32), 0.0),
@@ -203,29 +219,12 @@
     def masked(v):
         return jnp.where(inside_all, v, 0.0)
 
-    wrow = [
-        jnp.concatenate([wf[2 * k : 2 * k + 1, :], wf[2 * k + 1 : 2 * k + 2, :]], axis=1) for k in range(PK)
-    ]
-    low = jnp.where(has_low, hcot[0], 0.0)
-    high = jnp.where(has_high, hcot[1], 0.0)
-    line = jnp.concatenate([low, cot[...], high], axis=1)
-    cots[...] = jnp.zeros_like(cots)
-    wfs[...] = jnp.zeros_like(wfs)
-    pieces = split3(line)
-    for p in range(3):
-        for k in range(PK):
-            start = FRAMES - HALO - k + 1
-            cots[3 * k + p : 3 * k + p + 1, :] = pltpu.roll(pieces[p], 3 * FRAMES - start, 1)[:, : 2 * FRAMES]
-            wfs[3 * k + p : 3 * k + p + 1, :] = wrow[k].astype(F32)
-        cots[16 + p : 17 + p, 0:FRAMES] = pieces[p][:, FRAMES : 2 * FRAMES]
-    upstream = dot(cots[0:16].astype(BF16), wfs[...].astype(BF16), 0, 0)[:ROWS]
-    hear(5, 6, 7, 8)
-    tell((9, y_up), (10, z_up))
     delta = masked(upstream * slope3).astype(BF16)
     grad = dot(x3[...], delta[OWN], 0, 0)
     g3s[0], g3s[1] = grad[:, :128], grad[:, 128:]
     plane = NX * NY
-    for h in range(CORES):
+    halves = (1 - core, core)
+    for h in halves:
         for a in range(ZL):
             for r in range(AR):
                 ast.at[h][pl.ds(a * AR + r, plane, stride=ZL * AR), :] = g3s.at[h][
@@ -233,7 +232,11 @@
                 ]
         for x in range(NX):
             ab[h, x] = ast[h, x * NY * ZL * AR : (x + 1) * NY * ZL * AR].astype(BF16)
-    core_a = send(ab.at[1 - core], a0, s0.at[0], q0.at[0], partner)
+        if h is halves[0]:
+            core_a = send(ab.at[h], a0, s0.at[0], q0.at[0], partner)
+
+    hear(5, 6, 7, 8)
+    tell((9, y_up), (10, z_up))
 
     def back(delta, weight, width):
         d = delta.astype(F32)
@@ -249,8 +252,8 @@
     upstream = back(delta, w3, C2)
     delta = masked(upstream * slope2).astype(BF16)
     grad = dot(x2[...], delta[OWN], 0, 0)
+    g2s[0], g2s[1] = grad[:, :128], grad[:, 128:]
     for h in range(CORES):
-        g2s[h] = grad[:, h * 128 : (h + 1) * 128]
         for r in range(CR):
             cst.at[h][pl.ds(r, SHARES, stride=CR), :] = g2s.at[h][pl.ds(r, SHARES, stride=SECOND), :]
         cb[h] = cst[h].astype(BF16).reshape(ZL, NX, NY * CR, 128)
@@ -325,7 +328,6 @@
             acc = acc + arrived[d].astype(F32)
         return acc
 
-    hear(9, 10)
     core_a.wait_recv()
     a1[...] = (ab[core].astype(F32) + a0[...].astype(F32)).astype(BF16)
     a_x = along_x(a1, ax, sax, qax)
@@ -333,6 +335,7 @@
     c1[...] = (cb[core].astype(F32) + c0[...].astype(F32)).astype(BF16)
     pair = pz + 1 - 2 * zl
     c_z = send(c1.at[1 - zl], cz, scz, qcz, at(z=pair))
+    hear(9, 10)
     core_b.wait_recv()
     b1[...] = (bb[core].astype(F32) + b0[...].astype(F32)).astype(BF16)
     b_y = along_y(b1, by, sby, qby)
@@ -347,10 +350,10 @@
     c_x = along_x(c2, cx, scx, qcx)
     a2[...] = gathered(a_x, a1[px], ax).astype(BF16).reshape(NY, ZL * AR, 128)
     a_y = along_y(a2, ay, say, qay)
+    c3[...] = gathered(c_x, c2[px], cx).astype(BF16).reshape(NY, CR, 128)
+    c_y = along_y(c3, cy, scy, qcy)
     b2[...] = gathered(b_y, b1[py], by).astype(BF16).reshape(NX, ZL * BR, 128)
     b_x = along_x(b2, bx, sbx, qbx)
-    c3[...] = gathered(c_x, c2[px], cx).astype(BF16).reshape(NY, CR, 128)
-    c_y = along_y(c3, cy, scy, qcy)
 
     zf[...] = jnp.zeros_like(zf)
     total = gathered(b_x, b2[px], bx)

time: 41.8 us -> 41.9 us (level)
  no operation moved by 1% of the time
where the time goes in v5:
time: 41.9 us; the launch traced here: 41.8 us
  Pallas kernels  41.1 us (98%)
  between operations  0.64 us (2%)
    pallas_call x1, Pallas kernels, shards(): pl.pallas_call(kernel, out_shape=(jax.ShapeDtypeStruct((1, FRAMES), F32),...  40.4 us

profile of v5, /device:TPU:1, one launch (start us, length us, event | category | flops | bytes accessed | tf_op | source)
XLA Modules:
  0.0 41.8 jit_solution(11534415303878609843)
XLA Ops:
  0.6 40.4 %shard_map.135 = (f32[1,128]{1,0:T(1,128)S(1)}, f32[1,128,512]{2,1,0:T(8,128)S(1)}, f32[2,40,128]{2,1,0:T(8,128)S(1)}) custom-call(bf16[1,128,512]{2,1,0:T(8,128)(2,1)} %feat_in.1, f32[1,128]{1,0:T(1,128)} %cot_in.1, bf16[512,768]{1,0:T(8,128)(2,1)} %wp_in.1, bf16[64,768]{1,0:T(8,128)(2,1)} %ws_in.1, bf16[320,128]{1,0:T(8,128)(2,1)} %w1_in.1, ...), custom_call_target="tpu_custom_call" | custom-call | tf_op jit(solution)/shard_map/pallas_call | solution.py:411
  41.0 0.7 %shard_map.136 = (f32[1,128]{1,0:T(1,128)}, f32[1,128,512]{2,1,0:T(8,128)}, f32[1,768]{1,0:T(1,128)}, f32[5,128]{1,0:T(8,128)}, f32[10,256]{1,0:T(8,128)}, /*index=5*/f32[20,256]{1,0:T(8,128)}, f32[12]{0:T(128)}) custom-call(f32[1,128]{1,0:T(1,128)S(1)} %get-tuple-element.10.scores_in, f32[1,128,512]{2,1,0:T(8,128)S(1)} %get-tuple-element.11.fgrad_in, ...), custom_call_target="tpu_custom_call" | custom-call | tf_op jit(solution)/shard_map/pallas_call | solution.py:484

commit v6 on v5

--- a/solution.py
+++ b/solution.py
@@ -65,7 +65,8 @@
 
 def kernel(
     feat_in, cot_in, wp_in, ws_in, w1_in, w2_in, w3_in, wf_in,
-    scores, fgrad, fin_out,
+    scores, fgrad_out, fin_out,
+    fgrad, out_sem,
     feat, cot, wp, ws, w1, w2, w3, wf, in_sem,
     hfeat, hcot, x1, x2, x3, cots, wfs, g3s, g2s, g1s, ast, cst, bst,
     ab, a0, a1, ax, a2, ay, cb, c0, c1, cz, c2, cx, c3, cy, bb, b0, b1, by, b2, bx,
@@ -344,6 +345,8 @@
     projected_grad = normalize_back(hidden_upstream, hidden_normed, hidden_inverse).astype(BF16)
     normed_grad = dot(projected_grad, wp[...], 1, 1)
     fgrad[0] = normalize_back(normed_grad, normed_in, inverse_in)
+    written = pltpu.make_async_copy(fgrad, fgrad_out, out_sem)
+    written.start()
 
     c_z.wait_recv()
     c2[...] = (c1[zl].astype(F32) + cz[...].astype(F32)).astype(BF16)
@@ -387,13 +390,14 @@
     send(fin.at[core], fin.at[core], s4, q4, partner).wait_recv()
 
     fin_out[...] = fin[...]
+    written.wait()
     for copy in sent:
         copy.wait_send()
 
 
 def finish(scores_in, fgrad_in, fin, scores, fgrad, sq_out, g1_out, g2_out, g3_out, gf_out):
+    fgrad[...] = fgrad_in[...]
     scores[...] = scores_in[...]
-    fgrad[...] = fgrad_in[...]
     g3_out[...] = jnp.concatenate([fin[0, 0:20], fin[1, 0:20]], axis=1)
     for h in range(CORES):
         g2_out[0:CR, h * 128 : (h + 1) * 128] = fin[h, 32:40]
@@ -416,8 +420,10 @@
             jax.ShapeDtypeStruct((2, 40, 128), F32),
         ),
         in_specs=[pl.BlockSpec(memory_space=pltpu.HBM)] * 8,
-        out_specs=(vmem,) * 3,
+        out_specs=(vmem, pl.BlockSpec(memory_space=pl.ANY), vmem),
         scratch_shapes=[
+            pltpu.VMEM((1, FRAMES, 512), F32),
+            dma,
             pltpu.VMEM((FRAMES, 512), BF16),
             pltpu.VMEM((1, FRAMES), F32),
             pltpu.VMEM((512, 768), BF16),

time: 41.9 us -> 41.9 us (level)
  no operation moved by 1% of the time
where the time goes in v6:
time: 41.9 us; the launch traced here: 41.8 us
  Pallas kernels  41.2 us (98%)
  between operations  0.64 us (2%)
    pallas_call x1, Pallas kernels, shards(): pl.pallas_call(kernel, out_shape=(jax.ShapeDtypeStruct((1, FRAMES), F32),...  40.4 us

profile of v6, /device:TPU:1, one launch (start us, length us, event | category | flops | bytes accessed | tf_op | source)
XLA Modules:
  0.0 41.8 jit_solution(3041904968028504991)
XLA Ops:
  0.6 40.4 %shard_map.135 = (f32[1,128]{1,0:T(1,128)S(1)}, f32[1,128,512]{2,1,0:T(8,128)S(1)}, f32[2,40,128]{2,1,0:T(8,128)S(1)}) custom-call(bf16[1,128,512]{2,1,0:T(8,128)(2,1)} %feat_in.1, f32[1,128]{1,0:T(1,128)} %cot_in.1, bf16[512,768]{1,0:T(8,128)(2,1)} %wp_in.1, bf16[64,768]{1,0:T(8,128)(2,1)} %ws_in.1, bf16[320,128]{1,0:T(8,128)(2,1)} %w1_in.1, ...), custom_call_target="tpu_custom_call" | custom-call | tf_op jit(solution)/shard_map/pallas_call | solution.py:415
  41.1 0.7 %shard_map.136 = (f32[1,128]{1,0:T(1,128)}, f32[1,128,512]{2,1,0:T(8,128)}, f32[1,768]{1,0:T(1,128)}, f32[5,128]{1,0:T(8,128)}, f32[10,256]{1,0:T(8,128)}, /*index=5*/f32[20,256]{1,0:T(8,128)}, f32[12]{0:T(128)}) custom-call(f32[1,128]{1,0:T(1,128)S(1)} %get-tuple-element.10.scores_in, f32[1,128,512]{2,1,0:T(8,128)S(1)} %get-tuple-element.11.fgrad_in, ...), custom_call_target="tpu_custom_call" | custom-call | tf_op jit(solution)/shard_map/pallas_call | solution.py:490
